TPU v7x, 128 devices: a whole 4x4x4 slice. The times are simulated.
128 devices in a mesh: row: 8 (over y, core), col: 16 (over x, z).
Axes of the slice: x: 4, y: 4, z: 4, core: 2. Of those that a mesh axis runs over, the one named last changes fastest.
Arguments:
- user_emb: float32 [8, 16, 2048, 128], P('row', 'col'), may hold values from -2.4 to 2.4
- item_emb: float32 [16, 8, 1024, 128], P('col', 'row'), may hold values from -2.4 to 2.4
- tile_vals: bfloat16 [8, 16, 512, 128, 128], P('row', 'col'), may hold values from 0 to 0.029907227
- tile_rows: int32 [8, 16, 512], P('row', 'col'), may hold values from 0 to 255
- tile_cols: int32 [8, 16, 512], P('row', 'col'), may hold values from 0 to 63
- tile_count: int32 [8, 16], P('row', 'col'), may hold values from 128 to 512, as said below
- pair_users: int32 [65536], P(('row', 'col')), may hold values from 0 to 262143, as said below
- pair_items: int32 [65536], P(('row', 'col')), may hold values from 0 to 131071, as said below
- negatives: int32 [1024], replicated, may hold values from 0 to 131071, as said below
Outputs:
- user_final: float32 [8, 16, 2048, 128], P('row', 'col')
- item_final: float32 [16, 8, 1024, 128], P('col', 'row')
- bpr_terms: float32 [65536, 1024], P(('row', 'col'))
Inputs may be any that keep to these rules, and one draw needn't show every extreme that they name: `pair_users`: taken in aligned blocks of 512 entries, at most 8 entries of one block name users that one device holds in user_emb; in every draw some device's users are named exactly 8 times in every block. `pair_items`: taken in aligned blocks of 512 entries, at most 8 entries of one block name items that one device holds in item_emb; in every draw some device's items are named exactly 8 times in every block. `tile_count`: some block has all 512 slots live. `negatives`: entry j names an item that the device with row index (j // 8) // 16 and col index (j // 8) % 16 holds in item_emb.
All inputs are finite; a program needn't handle non-finite values.
Results may differ from a plain program's by a relative error of at most 0.009.
Values may be sent and summed in bfloat16 or wider, within the bound.
A program may use at most 128 MiB of HBM per device.

v0:
```python
import math

import jax
import jax.numpy as jnp
from jax import lax
from jax.sharding import Mesh
from jax.sharding import PartitionSpec as P

ROW = ("row_0", "row_1")
COL = ("col_0", "col_1")
ROW_COL = ("row_0", "row_1", "col_0", "col_1")


def from_everyone(array, axis):
    copies = jnp.broadcast_to(array, (lax.axis_size(axis), *array.shape))
    return lax.all_to_all(copies, axis, split_axis=0, concat_axis=0, tiled=True)


def in_order(blocks, dim):
    blocks = jnp.moveaxis(blocks, 0, dim)
    shape = blocks.shape
    return blocks.reshape(*shape[:dim], shape[dim] * shape[dim + 1], *shape[dim + 2 :])


def collect(array, axis, dim):
    blocks = from_everyone(array, axis)
    return in_order(blocks, dim)


def in_blocks(array, dim, length):
    shape = array.shape
    blocks = array.reshape(*shape[:dim], length, shape[dim] // length, *shape[dim + 1 :])
    return jnp.moveaxis(blocks, dim, 0)


def sent_and_summed(array, axis, dim):
    blocks = in_blocks(array, dim, lax.axis_size(axis))
    arrived = lax.all_to_all(blocks, axis, split_axis=0, concat_axis=0, tiled=True)
    return arrived.astype(jnp.float32).sum(axis=0)


def gather_in_order(array, axes, sequence):
    blocks = array[None]
    for k in sequence:
        blocks = lax.all_gather(blocks, axes[k], axis=0, tiled=True)
    held = [lax.axis_size(axes[k]) for k in reversed(sequence)]
    blocks = blocks.reshape(*held, *array.shape)
    turned = sorted(range(len(sequence)), key=lambda place: sequence[len(sequence) - 1 - place])
    return blocks.transpose(*turned, *range(len(sequence), blocks.ndim)).reshape(-1, *array.shape)


def whole_of(array, axes, sequence, dim):
    return in_order(gather_in_order(array, axes, sequence), dim)


def tile_products(values_all, row_all, col_all, number, user_tiles, item_tiles):
    total = values_all.shape[0]
    width = math.gcd(total, 64)
    blocks = (number + width - 1) // width

    def advance(block_index, totals):
        user_part, item_part = totals
        offset = block_index * width
        values = lax.dynamic_slice_in_dim(values_all, offset, width, 0)
        row_ids = lax.dynamic_slice_in_dim(row_all, offset, width, 0)
        col_ids = lax.dynamic_slice_in_dim(col_all, offset, width, 0)
        live_mask = (offset + jnp.arange(width, dtype=jnp.int32) < number).astype(jnp.float32)[
            :, None, None
        ]
        to_users = (
            jnp.einsum(
                "tij,tje->tie", values, item_tiles[col_ids], preferred_element_type=jnp.float32
            )
            * live_mask
        )
        to_items = (
            jnp.einsum(
                "tij,tie->tje", values, user_tiles[row_ids], preferred_element_type=jnp.float32
            )
            * live_mask
        )
        return (user_part.at[row_ids].add(to_users), item_part.at[col_ids].add(to_items))

    start = (jnp.zeros(user_tiles.shape, jnp.float32), jnp.zeros(item_tiles.shape, jnp.float32))
    return lax.fori_loop(0, blocks, advance, start)


def place_requests(owner, local, devices, slots_per):
    hits = (owner[:, None] == jnp.arange(devices, dtype=jnp.int32)[None, :]).astype(jnp.int32)
    rank = jnp.sum((jnp.cumsum(hits, axis=0) - 1) * hits, axis=1)
    slot = owner * slots_per + rank
    request = jnp.zeros((devices * slots_per,), jnp.int32).at[slot].set(local)
    return (slot, request.reshape(devices, slots_per))


def on_device(
    user_emb,
    item_emb,
    tile_vals,
    tile_rows,
    tile_cols,
    tile_count,
    pair_users,
    pair_items,
    negatives,
):
    row_count = lax.axis_size(ROW)
    col_count = lax.axis_size(COL)
    user_dev = user_emb.shape[2]
    item_dev = item_emb.shape[2]
    embed = user_emb.shape[3]
    tile_side = tile_vals.shape[-1]
    user_whole = lax.all_gather(user_emb.astype(jnp.bfloat16), COL, axis=1, tiled=True)
    item_whole = collect(item_emb.astype(jnp.bfloat16), ROW, 1)
    user_tiles = user_whole.reshape(-1, tile_side, embed)
    item_tiles = item_whole.reshape(-1, tile_side, embed)
    user_part, item_part = tile_products(
        tile_vals[0, 0], tile_rows[0, 0], tile_cols[0, 0], tile_count[0, 0], user_tiles, item_tiles
    )
    user_prop = lax.psum_scatter(
        user_part.reshape(-1, embed).astype(jnp.bfloat16), COL, scatter_dimension=0, tiled=True
    ).astype(jnp.float32)
    item_prop = sent_and_summed(item_part.reshape(-1, embed).astype(jnp.bfloat16), ROW, 0)
    user_final = (user_emb[0, 0] + user_prop) * 0.5
    item_final = (item_emb[0, 0] + item_prop) * 0.5
    devices = row_count * col_count
    slots_per = 2 * pair_users.shape[0] // devices
    user_owner = pair_users // user_dev
    user_local = pair_users % user_dev
    item_holder = pair_items // item_dev
    item_owner = item_holder % row_count * col_count + item_holder // row_count
    item_local = pair_items % item_dev
    user_slot, user_request = place_requests(user_owner, user_local, devices, slots_per)
    item_slot, item_request = place_requests(item_owner, item_local, devices, slots_per)
    user_wanted = lax.all_to_all(user_request, ROW_COL, split_axis=0, concat_axis=0, tiled=True)
    item_wanted = lax.all_to_all(item_request, ROW_COL, split_axis=0, concat_axis=0, tiled=True)
    user_rows = lax.all_to_all(
        user_final[user_wanted].astype(jnp.bfloat16),
        ROW_COL,
        split_axis=0,
        concat_axis=0,
        tiled=True,
    ).astype(jnp.float32)
    item_rows = lax.all_to_all(
        item_final[item_wanted].astype(jnp.bfloat16),
        ROW_COL,
        split_axis=0,
        concat_axis=0,
        tiled=True,
    ).astype(jnp.float32)
    user_vec = user_rows.reshape(-1, embed)[user_slot]
    item_vec = item_rows.reshape(-1, embed)[item_slot]
    offset = (lax.axis_index(COL) * row_count + lax.axis_index(ROW)) * item_dev
    neg_each = negatives.shape[0] // devices
    device_rank = lax.axis_index(ROW) * col_count + lax.axis_index(COL)
    mine = lax.dynamic_slice_in_dim(negatives, device_rank * neg_each, neg_each, 0) - offset
    negative_vec = whole_of(item_final[mine], ROW_COL, (0, 2, 3, 1), 0)
    positive = jnp.sum(user_vec * item_vec, axis=1)
    against = jnp.dot(user_vec, negative_vec.T, precision=lax.Precision.HIGHEST)
    bpr_terms = jnp.log1p(jnp.exp(against - positive[:, None]))
    return (user_final.reshape(user_emb.shape), item_final.reshape(item_emb.shape), bpr_terms)


def solution(mesh):
    torus = Mesh(mesh.devices.reshape(4, 2, 4, 4), ("row_0", "row_1", "col_0", "col_1"))
    return jax.shard_map(
        on_device,
        mesh=torus,
        in_specs=(
            P(ROW, COL, None, None),
            P(COL, ROW, None, None),
            P(ROW, COL, None, None, None),
            P(ROW, COL, None),
            P(ROW, COL, None),
            P(ROW, COL),
            P(ROW_COL),
            P(ROW_COL),
            P(),
        ),
        out_specs=(P(ROW, COL, None, None), P(COL, ROW, None, None), P(ROW_COL, None)),
        check_vma=False,
    )
```

profile of v0, /device:TPU:1, one launch (start us, length us, event | category | flops | bytes accessed | tf_op | source)
XLA Modules:
  0.0 614.8 jit_solution(11518100190499439016)
XLA Ops:
  12.0 6.0 all-to-all-start
  18.6 25.5 %all-to-all-done = bf16[8,1,1,1024,128]{4,3,2,1,0:T(8,128)(2,1)S(1)} async-done(((bf16[8,1,1,1024,128]{4,3,2,1,0:T(8,128)(2,1)}), bf16[8,1,1,1024,128]{4,3,2,1,0:T(8,128)(2,1)S(1)}, u32[]{:S(2)}, u32[]{:S(2)}) %all-to-all-start) | async-done | bytes 2097184 | tf_op jit(solution)/shard_map/all_to_all | solution.py:16
  44.1 40.6 %all-gather.3.cloned.1.call-done = bf16[1,16,2048,128]{3,2,0,1:T(8,128)(2,1)} async-done(((bf16[1,1,2048,128]{3,2,0,1:T(8,128)(2,1)}), bf16[1,16,2048,128]{3,2,0,1:T(8,128)(2,1)}) %all-gather.3.cloned.1.call-update) | async-done | bytes 8388624 | tf_op jit(solution)/shard_map/all_gather | solution.py:113
  84.7 7.8 %broadcast_in_dim.23 = f32[256,128,128]{2,1,0:T(8,128)} broadcast(f32[]{:T(128)} %constant.123.clone.1), dimensions={} | broadcast | bytes 16777220 | tf_op jit(solution)/shard_map/broadcast_in_dim | solution.py:84
  95.0 134.9 %while.12 = (s32[]{:T(128)}, f32[256,128,128]{2,1,0:T(8,128)}, f32[64,128,128]{2,1,0:T(8,128)}, s32[]{:T(128)}, s32[512]{0:T(512)}, /*index=5*/bf16[512,128,128]...) while((s32[]{:T(128)}, f32[256,128,128]{2,1,0:T(8,128)}, ...), condition=%wide.region_3.4_spmd, body=%wide.region_0.3_spmd.sunk | while | flops 541067840 | bytes 67120640 | solution.py:85
  103.8 13.6 %scatter_fusion = f32[256,128,128]{2,1,0:T(8,128)} fusion(f32[256,128,128]{2,1,0:T(8,128)} %get-tuple-element.166, s32[64]{0:T(128)S(1)} %get-tuple-element.149, f32[64,128,128]{2,1,0:T(8,128)} %convolution_multiply_fusion.4), kind=kCustom, calls=%fused_computation.8.clone.1 | custom fusion | flops 1048576 | bytes 12583168 | tf_op jit(solution)/shard_map/while/body/scatter-add | solution.py:82
  126.3 13.7 %scatter_fusion.1 = f32[64,128,128]{2,1,0:T(8,128)} fusion(f32[64,128,128]{2,1,0:T(8,128)} %get-tuple-element.167, s32[64]{0:T(128)S(1)} %get-tuple-element.150, f32[64,128,128]{2,1,0:T(8,128)} %convolution_multiply_fusion.5), kind=kCustom, calls=%fused_computation.9.clone.1 | custom fusion | flops 1048576 | bytes 12583168 | tf_op jit(solution)/shard_map/while/body/scatter-add | solution.py:82
  148.8 13.6 %scatter_fusion = f32[256,128,128]{2,1,0:T(8,128)} fusion(f32[256,128,128]{2,1,0:T(8,128)} %get-tuple-element.166, s32[64]{0:T(128)S(1)} %get-tuple-element.149, f32[64,128,128]{2,1,0:T(8,128)} %convolution_multiply_fusion.4), kind=kCustom, calls=%fused_computation.8.clone.1 | custom fusion | flops 1048576 | bytes 12583168 | tf_op jit(solution)/shard_map/while/body/scatter-add | solution.py:82
  166.7 4.6 convolution_multiply_fusion.5
  171.3 13.6 %scatter_fusion.1 = f32[64,128,128]{2,1,0:T(8,128)} fusion(f32[64,128,128]{2,1,0:T(8,128)} %get-tuple-element.167, s32[64]{0:T(128)S(1)} %get-tuple-element.150, f32[64,128,128]{2,1,0:T(8,128)} %convolution_multiply_fusion.5), kind=kCustom, calls=%fused_computation.9.clone.1 | custom fusion | flops 1048576 | bytes 12583168 | tf_op jit(solution)/shard_map/while/body/scatter-add | solution.py:82
  193.7 13.7 %scatter_fusion = f32[256,128,128]{2,1,0:T(8,128)} fusion(f32[256,128,128]{2,1,0:T(8,128)} %get-tuple-element.166, s32[64]{0:T(128)S(1)} %get-tuple-element.149, f32[64,128,128]{2,1,0:T(8,128)} %convolution_multiply_fusion.4), kind=kCustom, calls=%fused_computation.8.clone.1 | custom fusion | flops 1048576 | bytes 12583168 | tf_op jit(solution)/shard_map/while/body/scatter-add | solution.py:82
  216.3 13.6 %scatter_fusion.1 = f32[64,128,128]{2,1,0:T(8,128)} fusion(f32[64,128,128]{2,1,0:T(8,128)} %get-tuple-element.167, s32[64]{0:T(128)S(1)} %get-tuple-element.150, f32[64,128,128]{2,1,0:T(8,128)} %convolution_multiply_fusion.5), kind=kCustom, calls=%fused_computation.9.clone.1 | custom fusion | flops 1048576 | bytes 12583168 | tf_op jit(solution)/shard_map/while/body/scatter-add | solution.py:82
  229.9 9.2 %convert_element_type.55 = bf16[256,128,128]{2,1,0:T(8,128)(2,1)} convert(f32[256,128,128]{2,1,0:T(8,128)} %get-tuple-element.57) | non-fusion elementwise | flops 4194304 | bytes 25165824 | tf_op jit(solution)/shard_map/convert_element_type | solution.py:121
  243.6 231.8 %all-to-all-start.2 = ((s32[128,1,8]{2,1,0:T(1,128)}), s32[128,1,8]{2,1,0:T(1,128)S(1)}, u32[]{:S(2)}, u32[]{:S(2)}) async-start(s32[128,1,8]{2,1,0:T(1,128)} %bitcast.17), calls=%async_computation.3 | async-start | bytes 131072 | tf_op jit(solution)/shard_map/all_to_all | solution.py:135
  479.4 5.6 all-to-all-done.2
  485.0 4.6 all-to-all-start.4
  493.6 5.6 all-to-all-done.4
  499.2 4.7 all-to-all-start.1
  505.0 25.2 %all-to-all-done.1 = bf16[8,1024,128]{2,1,0:T(8,128)(2,1)S(1)} async-done(((bf16[8,1024,128]{2,1,0:T(8,128)(2,1)}), bf16[8,1024,128]{2,1,0:T(8,128)(2,1)S(1)}, u32[]{:S(2)}, u32[]{:S(2)}) %all-to-all-start.1) | async-done | bytes 2097184 | tf_op jit(solution)/shard_map/all_to_all | solution.py:38
  539.5 10.6 %all-gather = f32[32,128]{1,0:T(8,128)S(1)} all-gather(f32[8,128]{1,0:T(8,128)S(1)} %gather_fusion.4), channel_id=2, replica_groups=mesh['row_0'=4,'row_1'=2,'col_0'=4,'col_1'=4] {'row_0'}, dimensions={0}, use_global_device_ids=true | all-gather | bytes 20480 | tf_op jit(solution)/shard_map/all_gather | solution.py:45
  550.1 9.1 %all_gather.17 = f32[16,8,128]{2,1,0:T(8,128)S(1)} all-gather(f32[4,8,128]{2,1,0:T(8,128)S(1)} %bitcast.86), channel_id=1, replica_groups=mesh['row_0'=4,'row_1'=2,'col_0'=4,'col_1'=4] {'col_0'}, dimensions={0}, use_global_device_ids=true | all-gather | bytes 81920 | tf_op jit(solution)/shard_map/all_gather | solution.py:45
  559.3 10.1 %all_gather.18 = f32[64,8,128]{2,1,0:T(8,128)S(1)} all-gather(f32[16,8,128]{2,1,0:T(8,128)S(1)} %all_gather.17), channel_id=1, replica_groups=mesh['row_0'=4,'row_1'=2,'col_0'=4,'col_1'=4] {'col_1'}, dimensions={0}, use_global_device_ids=true | all-gather | bytes 327680 | tf_op jit(solution)/shard_map/all_gather | solution.py:45
  575.7 15.7 %all-to-all-start.3 = ((bf16[128,8,128]{2,1,0:T(8,128)(2,1)}), bf16[128,8,128]{2,1,0:T(8,128)(2,1)S(1)}, u32[]{:S(2)}, u32[]{:S(2)}) async-start(bf16[128,8,128]{2,1,0:T(8,128)(2,1)} %bitcast.66), calls=%async_computation.4 | async-start | bytes 524288 | tf_op jit(solution)/shard_map/all_to_all | solution.py:137
  595.5 6.8 %all-to-all-done.3 = bf16[128,8,128]{2,1,0:T(8,128)(2,1)S(1)} async-done(((bf16[128,8,128]{2,1,0:T(8,128)(2,1)}), bf16[128,8,128]{2,1,0:T(8,128)(2,1)S(1)}, u32[]{:S(2)}, u32[]{:S(2)}) %all-to-all-start.3) | async-done | bytes 262176 | tf_op jit(solution)/shard_map/all_to_all | solution.py:137
  (105 shorter events, 94.4 us)
Async XLA Ops:
  7.2 77.5 %all-gather.3.cloned.1.call-start = ((), (), s32[]{:S(2)}) async-start(), calls=%async_computation.7 | async-start | bytes 8912896 | tf_op jit(solution)/shard_map/all_gather | solution.py:113
  12.0 32.2 %all-to-all-start = ((bf16[8,1,1,1024,128]{4,3,2,1,0:T(8,128)(2,1)}), bf16[8,1,1,1024,128]{4,3,2,1,0:T(8,128)(2,1)S(1)}, u32[]{:S(2)}, u32[]{:S(2)}) async-start(bf16[8,1,1,1024,128]{4,3,2,1,0:T(8,128)(2,1)} %broadcast_in_dim.25), calls=%async_computation | async-start | bytes 4194304 | tf_op jit(solution)/shard_map/all_to_all | solution.py:16
  17.9 552.3 %reduce-scatter.2.cloned.1.call-start = ((), (), s32[]{:S(2)}) async-start(), calls=%async_computation.8 | async-start | bytes 8912896 | tf_op jit(solution)/shard_map/reduce_scatter | solution.py:120
  95.0 1.3 copy-start
  126.3 13.7 %copy-start.1 = (bf16[64,128,128]{2,1,0:T(8,128)(2,1)S(1)}, bf16[64,128,128]{2,1,0:T(8,128)(2,1)}, u32[]{:S(2)}) copy-start(bf16[64,128,128]{2,1,0:T(8,128)(2,1)} %copy-done) | copy-start | bytes 6291460 | tf_op jit(solution)/shard_map/while
  140.0 1.3 copy-start
  171.3 13.6 %copy-start.1 = (bf16[64,128,128]{2,1,0:T(8,128)(2,1)S(1)}, bf16[64,128,128]{2,1,0:T(8,128)(2,1)}, u32[]{:S(2)}) copy-start(bf16[64,128,128]{2,1,0:T(8,128)(2,1)} %copy-done) | copy-start | bytes 6291460 | tf_op jit(solution)/shard_map/while
  184.9 1.3 copy-start
  216.3 13.6 %copy-start.1 = (bf16[64,128,128]{2,1,0:T(8,128)(2,1)S(1)}, bf16[64,128,128]{2,1,0:T(8,128)(2,1)}, u32[]{:S(2)}) copy-start(bf16[64,128,128]{2,1,0:T(8,128)(2,1)} %copy-done) | copy-start | bytes 6291460 | tf_op jit(solution)/shard_map/while
  239.1 0.7 copy-start.4
  239.1 236.4 %copy-start.5 = (s32[512]{0:T(512)S(1)}, s32[512]{0:T(512)}, u32[]{:S(2)}) copy-start(s32[512]{0:T(512)} %param.18) | copy-start | bytes 6148
  243.6 241.4 %all-to-all-start.2 = ((s32[128,1,8]{2,1,0:T(1,128)}), s32[128,1,8]{2,1,0:T(1,128)S(1)}, u32[]{:S(2)}, u32[]{:S(2)}) async-start(s32[128,1,8]{2,1,0:T(1,128)} %bitcast.17), calls=%async_computation.3 | async-start | bytes 131072 | tf_op jit(solution)/shard_map/all_to_all | solution.py:135
  485.0 14.2 %all-to-all-start.4 = ((s32[128,1,8]{2,1,0:T(1,128)}), s32[128,1,8]{2,1,0:T(1,128)S(1)}, u32[]{:S(2)}, u32[]{:S(2)}) async-start(s32[128,1,8]{2,1,0:T(1,128)} %bitcast.30), calls=%async_computation.5 | async-start | bytes 131072 | tf_op jit(solution)/shard_map/all_to_all | solution.py:136
  493.6 36.9 %copy-start.3 = (f32[1,1,1024,128]{3,2,1,0:T(8,128)S(1)}, f32[1,1,1024,128]{3,2,1,0:T(8,128)}, u32[]{:S(2)}) copy-start(f32[1,1,1024,128]{3,2,1,0:T(8,128)} %param.12) | copy-start | bytes 1572868
  499.2 30.9 %all-to-all-start.1 = ((bf16[8,1024,128]{2,1,0:T(8,128)(2,1)}), bf16[8,1024,128]{2,1,0:T(8,128)(2,1)S(1)}, u32[]{:S(2)}, u32[]{:S(2)}) async-start(bf16[8,1024,128]{2,1,0:T(8,128)(2,1)} %bitcast.11), calls=%async_computation.2 | async-start | bytes 4194304 | tf_op jit(solution)/shard_map/all_to_all | solution.py:38
  534.6 41.2 %all-to-all-start.5 = ((bf16[128,8,128]{2,1,0:T(8,128)(2,1)}), bf16[128,8,128]{2,1,0:T(8,128)(2,1)S(1)}, u32[]{:S(2)}, u32[]{:S(2)}) async-start(bf16[128,8,128]{2,1,0:T(8,128)(2,1)} %bitcast.65), calls=%async_computation.6 | async-start | bytes 524288 | tf_op jit(solution)/shard_map/all_to_all | solution.py:144
  571.6 30.7 %copy-start.2 = (f32[2048,128]{1,0:T(8,128)}, f32[2048,128]{1,0:T(8,128)S(1)}, u32[]{:S(2)}) copy-start(f32[2048,128]{1,0:T(8,128)S(1)} %fusion.4) | copy-start | bytes 3145732
  575.7 26.5 %all-to-all-start.3 = ((bf16[128,8,128]{2,1,0:T(8,128)(2,1)}), bf16[128,8,128]{2,1,0:T(8,128)(2,1)S(1)}, u32[]{:S(2)}, u32[]{:S(2)}) async-start(bf16[128,8,128]{2,1,0:T(8,128)(2,1)} %bitcast.66), calls=%async_computation.4 | async-start | bytes 524288 | tf_op jit(solution)/shard_map/all_to_all | solution.py:137
Sparse Core Ops, SparseCore 0:
  10.7 73.9 all-gather.2
  239.2 311.1 reduce-scatter.1
where the time goes:
time: 619 us; the launch traced here: 615 us
  starting transfers between devices  267 us (43%)
  waiting for transfers between devices  109 us (18%)
  other arithmetic  107 us (17%)
  local copies, waits for them, and re-layouts  53.6 us (9%)
  blocking collectives  32.7 us (5%)
  matrix products  29.6 us (5%)
  between operations  15 us (2%)
    all_to_all x1, starting transfers between devices, on_device(): lax.all_to_all(user_request, ROW_COL, split_axis=0, concat_axis=0, tiled=...  232 us
    scatter-add x3, other arithmetic, advance(): user_part.at[row_ids].add(to_users)  40.9 us
    scatter-add x3, other arithmetic, advance(): item_part.at[col_ids].add(to_items)  40.8 us
    all_gather x1, waiting for transfers between devices, on_device(): lax.all_gather(user_emb.astype(jnp.bfloat16), COL, axis=1, tiled=True)  40.6 us
    all_gather x4, blocking collectives, gather_in_order(): blocks = lax.all_gather(blocks, axes[k], axis=0, tiled=True)  32.7 us
    all_to_all x1, waiting for transfers between devices, from_everyone(): return lax.all_to_all(copies, axis, split_axis=0, concat_axis=0, tiled=True)  25.5 us
    all_to_all x1, waiting for transfers between devices, sent_and_summed(): lax.all_to_all(blocks, axis, split_axis=0, concat_axis=0, tiled=True)  25.2 us
    all_to_all x1, starting transfers between devices, on_device(): lax.all_to_all(user_final[user_wanted].astype(jnp.bfloat16), ROW_COL, spl...  15.7 us
  transfers between devices with their start and end apart: 8, of which 6 were waited for; matrix products, arithmetic and copies ran while one was open for 4% of the time, Pallas kernels for 0%

commit v1 on v0

--- a/solution.py
+++ b/solution.py
@@ -1,8 +1,10 @@
-import math
+import functools
 
 import jax
 import jax.numpy as jnp
 from jax import lax
+from jax.experimental import pallas as pl
+from jax.experimental.pallas import tpu as pltpu
 from jax.sharding import Mesh
 from jax.sharding import PartitionSpec as P
 
@@ -53,36 +55,75 @@
     return in_order(gather_in_order(array, axes, sequence), dim)
 
 
-def tile_products(values_all, row_all, col_all, number, user_tiles, item_tiles):
-    total = values_all.shape[0]
-    width = math.gcd(total, 64)
-    blocks = (number + width - 1) // width
-
-    def advance(block_index, totals):
-        user_part, item_part = totals
-        offset = block_index * width
-        values = lax.dynamic_slice_in_dim(values_all, offset, width, 0)
-        row_ids = lax.dynamic_slice_in_dim(row_all, offset, width, 0)
-        col_ids = lax.dynamic_slice_in_dim(col_all, offset, width, 0)
-        live_mask = (offset + jnp.arange(width, dtype=jnp.int32) < number).astype(jnp.float32)[
-            :, None, None
-        ]
-        to_users = (
-            jnp.einsum(
-                "tij,tje->tie", values, item_tiles[col_ids], preferred_element_type=jnp.float32
-            )
-            * live_mask
-        )
-        to_items = (
-            jnp.einsum(
-                "tij,tie->tje", values, user_tiles[row_ids], preferred_element_type=jnp.float32
-            )
-            * live_mask
-        )
-        return (user_part.at[row_ids].add(to_users), item_part.at[col_ids].add(to_items))
-
-    start = (jnp.zeros(user_tiles.shape, jnp.float32), jnp.zeros(item_tiles.shape, jnp.float32))
-    return lax.fori_loop(0, blocks, advance, start)
+def tile_kernel(width, depth, users, count_ref, rows, cols, vals, table, out, acc, bufs, sems):
+    total = out.shape[0]
+    count = count_ref[0]
+    chunks = (count + width - 1) // width
+
+    def fetch(k, slot):
+        return pltpu.make_async_copy(vals.at[pl.ds(k * width, width)], bufs.at[slot], sems.at[slot])
+
+    for k in range(depth - 1):
+
+        @pl.when(k < chunks)
+        def _():
+            fetch(k, k).start()
+
+    @pl.loop(0, total + 1)
+    def _(i):
+        acc[i] = jnp.zeros(acc.shape[1:], jnp.float32)
+
+    @pl.loop(0, chunks)
+    def _(k):
+        slot = lax.rem(k, depth)
+        ahead = k + depth - 1
+
+        @pl.when(ahead < chunks)
+        def _():
+            fetch(ahead, lax.rem(ahead, depth)).start()
+
+        fetch(k, slot).wait()
+        products = []
+        for t in range(width):
+            spot = k * width + t
+            tile = bufs[slot, t]
+            if users:
+                left, right, place = tile, table[cols[spot]], rows[spot]
+            else:
+                left, right, place = table[rows[spot]], tile, cols[spot]
+            product = jnp.dot(left, right, preferred_element_type=jnp.float32)
+            products.append((jnp.where(spot < count, place, total), product))
+        for place, product in products:
+            acc[place] += product
+
+    @pl.loop(0, total)
+    def _(i):
+        tile = acc[i]
+        out[i] = (tile if users else tile.T).astype(jnp.bfloat16)
+
+
+def tile_terms(users, vals, rows, cols, count, table, total, width=16, depth=3):
+    slots, side, embed = *vals.shape[:2], table.shape[-1]
+    smem = pl.BlockSpec(memory_space=pltpu.SMEM)
+    vmem = pl.BlockSpec(memory_space=pltpu.VMEM)
+    return pl.pallas_call(
+        functools.partial(tile_kernel, width, depth, users),
+        name="user_terms" if users else "item_terms",
+        out_shape=jax.ShapeDtypeStruct((total, side, embed), jnp.bfloat16),
+        in_specs=[smem, smem, smem, pl.BlockSpec(memory_space=pl.ANY), vmem],
+        out_specs=vmem,
+        scratch_shapes=[
+            pltpu.VMEM((total + 1, side, embed), jnp.float32),
+            pltpu.VMEM((depth, width, side, side), jnp.bfloat16),
+            pltpu.SemaphoreType.DMA((depth,)),
+        ],
+        compiler_params=pltpu.CompilerParams(vmem_limit_bytes=56 * 2**20),
+        cost_estimate=pl.CostEstimate(
+            flops=slots * 2 * side * side * embed,
+            bytes_accessed=2 * (vals.size + table.size + total * side * embed),
+            transcendentals=0,
+        ),
+    )(count, rows, cols, vals, table)
 
 
 def place_requests(owner, local, devices, slots_per):
@@ -110,17 +151,17 @@
     item_dev = item_emb.shape[2]
     embed = user_emb.shape[3]
     tile_side = tile_vals.shape[-1]
-    user_whole = lax.all_gather(user_emb.astype(jnp.bfloat16), COL, axis=1, tiled=True)
+    user_turned = user_emb[0, 0].reshape(-1, tile_side, embed).swapaxes(1, 2)
+    user_tiles = lax.all_gather(user_turned.astype(jnp.bfloat16), COL, axis=0, tiled=True)
     item_whole = collect(item_emb.astype(jnp.bfloat16), ROW, 1)
-    user_tiles = user_whole.reshape(-1, tile_side, embed)
     item_tiles = item_whole.reshape(-1, tile_side, embed)
-    user_part, item_part = tile_products(
-        tile_vals[0, 0], tile_rows[0, 0], tile_cols[0, 0], tile_count[0, 0], user_tiles, item_tiles
-    )
+    slots = (tile_vals[0, 0], tile_rows[0, 0], tile_cols[0, 0], tile_count[0])
+    user_part = tile_terms(True, *slots, item_tiles, user_tiles.shape[0])
+    item_part = tile_terms(False, *slots, user_tiles, item_tiles.shape[0])
     user_prop = lax.psum_scatter(
-        user_part.reshape(-1, embed).astype(jnp.bfloat16), COL, scatter_dimension=0, tiled=True
+        user_part.reshape(-1, embed), COL, scatter_dimension=0, tiled=True
     ).astype(jnp.float32)
-    item_prop = sent_and_summed(item_part.reshape(-1, embed).astype(jnp.bfloat16), ROW, 0)
+    item_prop = sent_and_summed(item_part.reshape(-1, embed), ROW, 0)
     user_final = (user_emb[0, 0] + user_prop) * 0.5
     item_final = (item_emb[0, 0] + item_prop) * 0.5
     devices = row_count * col_count

time: 619 us -> 322 us (0.52)
  starting transfers between devices: 267 us -> 26.9 us
  other arithmetic: 107 us -> 5.81 us
  blocking collectives: 32.7 us -> 97.7 us
  Pallas kernels: 0 us -> 45.5 us
  local copies, waits for them, and re-layouts: 53.6 us -> 21.6 us
  matrix products: 29.6 us -> 3.06 us
    all_to_all x1, starting transfers between devices: 232 us -> 8.55 us  [on_device(): lax.all_to_all(user_request, ROW_COL, split_axis=0, concat_axis=0, tiled=...]
    scatter-add x6 -> x0, other arithmetic: 81.7 us -> none  [the longest x3 40.9 us: advance(): user_part.at[row_ids].add(to_users)]
    all_to_all x0 -> x2, blocking collectives: none -> 63.6 us  [the longest x1 33.2 us: sent_and_summed(): lax.all_to_all(blocks, axis, split_axis=0, concat_axis=0, tiled=True)]
    all_to_all x2 -> x0, waiting for transfers between devices: 50.7 us -> none  [the longest x1 25.5 us: from_everyone(): return lax.all_to_all(copies, axis, split_axis=0, concat_axis=0, tiled=True)]
    pallas_call x0 -> x2, Pallas kernels: none -> 45.5 us  [tile_terms(): pl.pallas_call(functools.partial(tile_kernel, width, depth, users), name=...]
    all_gather x1, waiting for transfers between devices: 40.6 us -> 74.5 us  [on_device(): lax.all_gather(user_turned.astype(jnp.bfloat16), COL, axis=0, tiled=True)]
    dot_general x6 -> x0, matrix products: 26.5 us -> none  [the longest x3 13.8 us: advance(): jnp.einsum('tij,tie->tje', values, user_tiles[row_ids], preferred_element...]
    gather x6 -> x0, local copies, waits for them, and re-layouts: 20.6 us -> none  [the longest x3 13 us: advance(): user_tiles[row_ids]]
  transfers between devices with their start and end apart: 8 -> 6, of which waited for: 6 -> 5; matrix products, arithmetic and copies ran while one was open for 4% -> 6% of each run, Pallas kernels for 0% -> 0%
where the time goes in v1:
time: 322 us; the launch traced here: 321 us
  waiting for transfers between devices  106 us (33%)
  blocking collectives  97.7 us (30%)
  Pallas kernels  45.5 us (14%)
  starting transfers between devices  26.9 us (8%)
  local copies, waits for them, and re-layouts  21.6 us (7%)
  between operations  15 us (5%)
  other arithmetic  5.81 us (2%)
    all_gather x1, waiting for transfers between devices, on_device(): lax.all_gather(user_turned.astype(jnp.bfloat16), COL, axis=0, tiled=True)  74.5 us
    pallas_call x2, Pallas kernels, tile_terms(): pl.pallas_call(functools.partial(tile_kernel, width, depth, users), name=...  45.5 us
    all_gather x4, blocking collectives, gather_in_order(): blocks = lax.all_gather(blocks, axes[k], axis=0, tiled=True)  34 us
    all_to_all x1, blocking collectives, sent_and_summed(): lax.all_to_all(blocks, axis, split_axis=0, concat_axis=0, tiled=True)  33.2 us
    all_to_all x1, blocking collectives, from_everyone(): return lax.all_to_all(copies, axis, split_axis=0, concat_axis=0, tiled=True)  30.4 us
    reduce_scatter x1, waiting for transfers between devices, on_device(): lax.psum_scatter(user_part.reshape(-1, embed), COL, scatter_dimension=0,...  10.5 us
    all_to_all x1, waiting for transfers between devices, on_device(): lax.all_to_all(item_request, ROW_COL, split_axis=0, concat_axis=0, tiled=...  9.42 us
    all_to_all x1, starting transfers between devices, on_device(): lax.all_to_all(user_final[user_wanted].astype(jnp.bfloat16), ROW_COL, spl...  8.63 us
  transfers between devices with their start and end apart: 6, of which 5 were waited for; matrix products, arithmetic and copies ran while one was open for 6% of the time, Pallas kernels for 0%

profile of v1, /device:TPU:1, one launch (start us, length us, event | category | flops | bytes accessed | tf_op | source)
XLA Modules:
  0.0 321.4 jit_solution(15504501048561471940)
XLA Ops:
  7.2 1.3 convert_element_type.41
  10.2 74.5 %all-gather.3.cloned.1.call-done.table = bf16[256,128,128]{2,1,0:T(8,128)(2,1)} async-done(((bf16[16,128,128]{2,1,0:T(8,128)(2,1)}), bf16[256,128,128]{2,1,0:T(8,128)(2,1)}) %all-gather.3.cloned.1.call-update) | async-done | bytes 8388624 | tf_op jit(solution)/shard_map/all_gather | solution.py:155
  84.7 24.6 %item_terms.1 = bf16[64,128,128]{2,1,0:T(8,128)(2,1)} custom-call(s32[1]{0:T(128)} %bitcast.70.count_ref, s32[512]{0:T(512)} %bitcast.86, s32[512]{0:T(512)} %bitcast.88, bf16[512,128,128]{2,1,0:T(8,128)(2,1)} %bitcast.71, bf16[256,128,128]{2,1,0:T(8,128)(2,1)} %all-gather.3.cloned.1.call-done.table), custom_call_target="tpu_custom_call" | custom-call | flops 2147483648 | bytes 27262976 | tf_op jit(solution)/shard_map/item_terms/pallas_call | solution.py:109
  109.3 33.2 %all_to_all.44 = bf16[8,1024,128]{2,1,0:T(8,128)(2,1)S(1)} all-to-all(bf16[8,1024,128]{2,1,0:T(8,128)(2,1)} %bitcast.77), channel_id=1, replica_groups=mesh['row_0'=4,'row_1'=2,'col_0'=4,'col_1'=4] {'row_0','row_1'}, dimensions={0} | all-to-all | bytes 4194304 | tf_op jit(solution)/shard_map/all_to_all | solution.py:40
  144.7 30.4 %all_to_all.45 = bf16[8,1,1,1024,128]{4,3,2,1,0:T(8,128)(2,1)} all-to-all(bf16[8,1,1,1024,128]{4,3,2,1,0:T(8,128)(2,1)S(1)} %broadcast_in_dim.10), channel_id=1, replica_groups=mesh['row_0'=4,'row_1'=2,'col_0'=4,'col_1'=4] {'row_0','row_1'}, dimensions={0} | all-to-all | bytes 4194304 | tf_op jit(solution)/shard_map/all_to_all | solution.py:18
  175.1 20.8 %user_terms.1 = bf16[256,128,128]{2,1,0:T(8,128)(2,1)} custom-call(s32[1]{0:T(128)} %bitcast.69.count_ref, s32[512]{0:T(512)} %bitcast.87, s32[512]{0:T(512)} %bitcast.89, bf16[512,128,128]{2,1,0:T(8,128)(2,1)} %bitcast.72, bf16[64,128,128]{2,1,0:T(8,128)(2,1)} %bitcast.76), custom_call_target="tpu_custom_call" | custom-call | flops 2147483648 | bytes 27262976 | tf_op jit(solution)/shard_map/user_terms/pallas_call | solution.py:109
  197.4 2.4 scatter_custom_fusion
  200.6 8.6 %all-to-all-start.2 = ((s32[128,1,8]{2,1,0:T(1,128)}), s32[128,1,8]{2,1,0:T(1,128)S(1)}, u32[]{:S(2)}, u32[]{:S(2)}) async-start(s32[128,1,8]{2,1,0:T(1,128)} %bitcast.17), calls=%async_computation.3 | async-start | bytes 131072 | tf_op jit(solution)/shard_map/all_to_all | solution.py:176
  210.7 2.4 scatter_custom_fusion.1
  213.8 4.8 %all-to-all-done.2 = s32[128,1,8]{2,1,0:T(1,128)S(1)} async-done(((s32[128,1,8]{2,1,0:T(1,128)}), s32[128,1,8]{2,1,0:T(1,128)S(1)}, u32[]{:S(2)}, u32[]{:S(2)}) %all-to-all-start.2) | async-done | bytes 4128 | tf_op jit(solution)/shard_map/all_to_all | solution.py:176
  218.6 5.0 %all-to-all-start.4 = ((s32[128,1,8]{2,1,0:T(1,128)}), s32[128,1,8]{2,1,0:T(1,128)S(1)}, u32[]{:S(2)}, u32[]{:S(2)}) async-start(s32[128,1,8]{2,1,0:T(1,128)} %bitcast.30), calls=%async_computation.5 | async-start | bytes 131072 | tf_op jit(solution)/shard_map/all_to_all | solution.py:177
  223.7 9.4 %all-to-all-done.4 = s32[128,1,8]{2,1,0:T(1,128)S(1)} async-done(((s32[128,1,8]{2,1,0:T(1,128)}), s32[128,1,8]{2,1,0:T(1,128)S(1)}, u32[]{:S(2)}, u32[]{:S(2)}) %all-to-all-start.4) | async-done | bytes 4128 | tf_op jit(solution)/shard_map/all_to_all | solution.py:177
  233.9 4.0 %gather_fusion.4 = bf16[1024,128]{1,0:T(8,128)(2,1)} fusion(f32[1024,128]{1,0:T(8,128)S(1)} %fusion.1, s32[1024]{0:T(1024)S(1)} %broadcast_clamp_fusion), kind=kCustom, calls=%fused_computation.4 | custom fusion | bytes 528384 | tf_op jit(solution)/shard_map/gather | solution.py:186
  237.9 4.7 %all-to-all-start.5 = ((bf16[128,8,128]{2,1,0:T(8,128)(2,1)}), bf16[128,8,128]{2,1,0:T(8,128)(2,1)S(1)}, u32[]{:S(2)}, u32[]{:S(2)}) async-start(bf16[128,8,128]{2,1,0:T(8,128)(2,1)} %bitcast.65), calls=%async_computation.6 | async-start | bytes 524288 | tf_op jit(solution)/shard_map/all_to_all | solution.py:185
  242.7 10.6 %all-gather = f32[32,128]{1,0:T(8,128)S(1)} all-gather(f32[8,128]{1,0:T(8,128)S(1)} %gather_fusion.2), channel_id=2, replica_groups=mesh['row_0'=4,'row_1'=2,'col_0'=4,'col_1'=4] {'row_0'}, dimensions={0}, use_global_device_ids=true | all-gather | bytes 20480 | tf_op jit(solution)/shard_map/all_gather | solution.py:47
  253.2 9.6 %all_gather.17 = f32[16,8,128]{2,1,0:T(8,128)S(1)} all-gather(f32[4,8,128]{2,1,0:T(8,128)S(1)} %bitcast.83), channel_id=1, replica_groups=mesh['row_0'=4,'row_1'=2,'col_0'=4,'col_1'=4] {'col_0'}, dimensions={0}, use_global_device_ids=true | all-gather | bytes 81920 | tf_op jit(solution)/shard_map/all_gather | solution.py:47
  262.9 10.8 %all_gather.18 = f32[64,8,128]{2,1,0:T(8,128)S(1)} all-gather(f32[16,8,128]{2,1,0:T(8,128)S(1)} %all_gather.17), channel_id=1, replica_groups=mesh['row_0'=4,'row_1'=2,'col_0'=4,'col_1'=4] {'col_1'}, dimensions={0}, use_global_device_ids=true | all-gather | bytes 327680 | tf_op jit(solution)/shard_map/all_gather | solution.py:47
  273.6 10.5 %reduce-scatter.2.cloned.1.call-done = bf16[2048,128]{1,0:T(8,128)(2,1)} async-done(((bf16[32768,128]{1,0:T(8,128)(2,1)}), bf16[2048,128]{1,0:T(8,128)(2,1)}) %reduce-scatter.2.cloned.1.call-update) | async-done | bytes 524304 | tf_op jit(solution)/shard_map/reduce_scatter | solution.py:161
  285.3 4.1 %gather_fusion = bf16[1024,128]{1,0:T(8,128)(2,1)} fusion(f32[2048,128]{1,0:T(8,128)S(1)} %fusion, s32[1024]{0:T(1024)S(1)} %broadcast_clamp_fusion.1), kind=kCustom, calls=%fused_computation | custom fusion | bytes 528384 | tf_op jit(solution)/shard_map/gather | solution.py:179
  289.4 8.6 %all-to-all-start.3 = ((bf16[128,8,128]{2,1,0:T(8,128)(2,1)}), bf16[128,8,128]{2,1,0:T(8,128)(2,1)S(1)}, u32[]{:S(2)}, u32[]{:S(2)}) async-start(bf16[128,8,128]{2,1,0:T(8,128)(2,1)} %bitcast.66), calls=%async_computation.4 | async-start | bytes 524288 | tf_op jit(solution)/shard_map/all_to_all | solution.py:178
  298.1 3.1 all_gather.19
  302.3 6.6 %all-to-all-done.3 = bf16[128,8,128]{2,1,0:T(8,128)(2,1)S(1)} async-done(((bf16[128,8,128]{2,1,0:T(8,128)(2,1)}), bf16[128,8,128]{2,1,0:T(8,128)(2,1)S(1)}, u32[]{:S(2)}, u32[]{:S(2)}) %all-to-all-start.3) | async-done | bytes 262176 | tf_op jit(solution)/shard_map/all_to_all | solution.py:178
  308.9 1.3 gather_fusion.1
  311.5 3.1 exponential_log-plus-one_fusion
  (60 shorter events, 11.9 us)
Async XLA Ops:
  7.2 77.5 %all-gather.3.cloned.1.call-start = ((), (), s32[]{:S(2)}) async-start(), calls=%async_computation.8 | async-start | bytes 8912896 | tf_op jit(solution)/shard_map/all_gather | solution.py:155
  9.5 274.6 %reduce-scatter.2.cloned.1.call-start = ((), (), s32[]{:S(2)}) async-start(), calls=%async_computation.7 | async-start | bytes 8912896 | tf_op jit(solution)/shard_map/reduce_scatter | solution.py:161
  142.6 1.0 copy-start.2
  196.0 0.7 copy-start.3
  196.0 13.1 %copy-start.4 = (s32[512]{0:T(512)S(1)}, s32[512]{0:T(512)}, u32[]{:S(2)}) copy-start(s32[512]{0:T(512)} %param.16) | copy-start | bytes 6148
  200.6 18.1 %all-to-all-start.2 = ((s32[128,1,8]{2,1,0:T(1,128)}), s32[128,1,8]{2,1,0:T(1,128)S(1)}, u32[]{:S(2)}, u32[]{:S(2)}) async-start(s32[128,1,8]{2,1,0:T(1,128)} %bitcast.17), calls=%async_computation.3 | async-start | bytes 131072 | tf_op jit(solution)/shard_map/all_to_all | solution.py:176
  218.6 14.5 %all-to-all-start.4 = ((s32[128,1,8]{2,1,0:T(1,128)}), s32[128,1,8]{2,1,0:T(1,128)S(1)}, u32[]{:S(2)}, u32[]{:S(2)}) async-start(s32[128,1,8]{2,1,0:T(1,128)} %bitcast.30), calls=%async_computation.5 | async-start | bytes 131072 | tf_op jit(solution)/shard_map/all_to_all | solution.py:177
  233.3 50.8 %copy-start.1 = (f32[1,1,2048,128]{3,2,1,0:T(8,128)S(1)}, f32[1,1,2048,128]{3,2,1,0:T(8,128)}, u32[]{:S(2)}) copy-start(f32[1,1,2048,128]{3,2,1,0:T(8,128)} %param.9) | copy-start | bytes 3145732
  237.9 51.5 %all-to-all-start.5 = ((bf16[128,8,128]{2,1,0:T(8,128)(2,1)}), bf16[128,8,128]{2,1,0:T(8,128)(2,1)S(1)}, u32[]{:S(2)}, u32[]{:S(2)}) async-start(bf16[128,8,128]{2,1,0:T(8,128)(2,1)} %bitcast.65), calls=%async_computation.6 | async-start | bytes 524288 | tf_op jit(solution)/shard_map/all_to_all | solution.py:185
  285.3 15.9 %copy-start = (f32[2048,128]{1,0:T(8,128)}, f32[2048,128]{1,0:T(8,128)S(1)}, u32[]{:S(2)}) copy-start(f32[2048,128]{1,0:T(8,128)S(1)} %fusion) | copy-start | bytes 3145732
  289.4 19.5 %all-to-all-start.3 = ((bf16[128,8,128]{2,1,0:T(8,128)(2,1)}), bf16[128,8,128]{2,1,0:T(8,128)(2,1)S(1)}, u32[]{:S(2)}, u32[]{:S(2)}) async-start(bf16[128,8,128]{2,1,0:T(8,128)(2,1)} %bitcast.66), calls=%async_computation.4 | async-start | bytes 524288 | tf_op jit(solution)/shard_map/all_to_all | solution.py:178
Sparse Core Ops, SparseCore 0:
  10.7 73.9 all-gather.2
  196.2 87.9 reduce-scatter.1

commit v2 on v1

v2 whole, which is shorter than its diff:
```python
import functools

import jax
import jax.numpy as jnp
from jax import lax
from jax.experimental import pallas as pl
from jax.experimental.pallas import tpu as pltpu
from jax.sharding import Mesh
from jax.sharding import PartitionSpec as P

ROW = ("row_0", "row_1")
COL = ("col_0", "col_1")
Y, CORE, X, Z = "row_0", "row_1", "col_0", "col_1"
SIDE = 4
ANY = pl.BlockSpec(memory_space=pl.ANY)
VMEM = pl.BlockSpec(memory_space=pltpu.VMEM)
SMEM = pl.BlockSpec(memory_space=pltpu.SMEM)
DMA = pltpu.SemaphoreType.DMA
ROW_COL = ("row_0", "row_1", "col_0", "col_1")


def greet(peers):
    barrier = pltpu.get_barrier_semaphore()
    for peer in peers:
        pl.semaphore_signal(barrier, inc=1, device_id=peer)
    return lambda: pl.semaphore_wait(barrier, len(peers))


def ahead(axis, step):
    return lax.rem(lax.axis_index(axis) + step, SIDE)


def slots_of(pairs, width, turn, devices, each, slot_out):
    count = pairs.shape[1]
    shift = width.bit_length() - 1
    holder = pairs >> shift
    owner = lax.rem(holder, 8) * 16 + holder // 8 if turn else holder
    local = pairs & (width - 1)
    owner_down = jnp.broadcast_to(owner, (128, count)).T[:, :1]
    below = lax.broadcasted_iota(jnp.int32, (count, count), 0)
    right = lax.broadcasted_iota(jnp.int32, (count, count), 1)
    same = owner_down == owner
    before = jnp.where(same & (below < right), 1, 0)
    after = jnp.where(same & (right < below), 1, 0)
    slot = owner * each + jnp.sum(before, axis=0, keepdims=True)
    slot_out[...] = owner_down * each + jnp.sum(after, axis=1, keepdims=True)
    first = lax.broadcasted_iota(jnp.int32, (devices, count), 0) * each
    return [
        jnp.sum(jnp.where(slot == first + k, local, 0), axis=1, keepdims=True) for k in range(each)
    ]


def first_gather_kernel(
    widths, item_emb, user_emb, pair_users, pair_items, items_out, x_out, z_out, user_slot, item_slot, request,
    items, users, table, sent, came, kept,
):
    y, core, x, z = (lax.axis_index(a) for a in (Y, CORE, X, Z))
    shard, half = items.shape[0], users.shape[0] // 2
    other = {CORE: 1 - core}
    steps = range(1, SIDE)
    entered = greet([other] + [{a: ahead(a, s)} for a in (Y, X, Z) for s in steps])
    tile = items.shape[1]
    for i in range(shard):
        items[i] = item_emb[pl.ds(i * tile, tile)].astype(jnp.bfloat16)
    for i in range(2 * half):
        users[i] = user_emb[pl.ds(i * tile, tile)].T.astype(jnp.bfloat16)
    entered()

    def place(y_of, core_of):
        return items_out.at[pl.ds((y_of * 2 + core_of) * shard, shard)]

    def send(k, src, dst, peer):
        copy = pltpu.make_async_remote_copy(src, dst, sent.at[k], came.at[k], device_id=peer)
        copy.start()
        return copy

    copies = []
    to_y = [send(s - 1, items, place(y, core), {Y: ahead(Y, s)}) for s in steps]
    copies.append(send(3, items, place(y, core), other))
    for s in steps:
        copies.append(send(6 + s, users.at[pl.ds(0, half)], x_out.at[x], {X: ahead(X, s)}))
        copies.append(send(9 + s, users.at[pl.ds(half, half)], z_out.at[z], {Z: ahead(Z, s)}))
    local = [
        pltpu.make_async_copy(items, place(y, core), kept.at[0]),
        pltpu.make_async_copy(users.at[pl.ds(0, half)], x_out.at[x], kept.at[1]),
        pltpu.make_async_copy(users.at[pl.ds(half, half)], z_out.at[z], kept.at[2]),
    ]
    for copy in local:
        copy.start()

    devices = request.shape[0]
    each = 2 * pair_users.shape[1] // devices
    wanted = slots_of(pair_users[...], widths[0], False, devices, each, user_slot)
    wanted += slots_of(pair_items[...], widths[1], True, devices, each, item_slot)
    lane = lax.broadcasted_iota(jnp.int32, table.shape, 1)
    spread = jnp.zeros(table.shape, jnp.int32)
    for k, column in enumerate(wanted):
        spread = jnp.where(lane == k, column, spread)
    table[...] = spread

    @pl.loop(0, devices)
    def _(d):
        request[d] = table[pl.ds(d, 1)]

    for s in steps:
        to_y[s - 1].wait()
        back = lax.rem(y + SIDE - s, SIDE)
        copies.append(send(3 + s, place(back, core), place(back, core), other))
    for copy in copies + local:
        copy.wait()


def first_gather(item_emb, user_emb, tile, pair_users, pair_items, widths, devices):
    shard, side = item_emb.shape[0] // tile, (tile, item_emb.shape[1])
    half, count = user_emb.shape[0] // tile // 2, pair_users.shape[1]
    stage = jax.ShapeDtypeStruct((SIDE, half, *side), jnp.bfloat16)
    slot = jax.ShapeDtypeStruct((count, 1), jnp.int32)
    return pl.pallas_call(
        functools.partial(first_gather_kernel, widths),
        name="first_gather",
        out_shape=(
            jax.ShapeDtypeStruct((8 * shard, *side), jnp.bfloat16), stage, stage,
            slot, slot, jax.ShapeDtypeStruct((devices, 1, 128), jnp.int32),
        ),
        in_specs=[VMEM] * 4,
        out_specs=(ANY, ANY, ANY, VMEM, VMEM, VMEM),
        scratch_shapes=[
            pltpu.VMEM((shard, *side), jnp.bfloat16), pltpu.VMEM((2 * half, *side), jnp.bfloat16),
            pltpu.VMEM((devices, 128), jnp.int32), DMA((13,)), DMA((13,)), DMA((3,)),
        ],
        compiler_params=pltpu.CompilerParams(
            collective_id=0, has_side_effects=True, vmem_limit_bytes=58 * 2**20
        ),
    )(item_emb, user_emb, pair_users, pair_items)


def shifted(array, axis, step):
    return lax.ppermute(array, axis, [(i, (i + step) % SIDE) for i in range(SIDE)])


def coords(rank):
    return {Y: rank // 32, CORE: lax.rem(rank // 16, 2), X: lax.rem(rank // 4, 4), Z: lax.rem(rank, 4)}


def settle_kernel(
    devices, each,
    x_own, x_up, x_down, z_own, z_up, z_down, items, user_emb, item_emb, request, user_slot, item_slot, negatives,
    user_out, item_out, margin,
    got_x, got_z, sum_x, sum_z, last_x, last_z, got_i, sum_i, last_i, asked, wanted, stage, packs, arrived,
    sent, came, kept, ready, ask_sent, ask_came, row_sent, row_came,
):
    y, core, x, z = (lax.axis_index(a) for a in (Y, CORE, X, Z))
    me = ((y * 2 + core) * SIDE + x) * SIDE + z
    steps = range(1, SIDE)
    half, tile = got_x.shape[2], got_x.shape[3]
    mates = [{Y: ahead(Y, s), CORE: lax.rem(core + c, 2)} for s in range(SIDE) for c in range(2) if s or c]
    entered = greet([{a: ahead(a, s)} for a in (X, Z) for s in steps] + mates)

    def other(s):
        return lax.rem(me + s, devices)

    def to_others(act, group=8):
        act(list(range(1, group)))

        @pl.loop(1, devices // group)
        def _(g):
            act([g * group + k for k in range(group)])

    loads = [pltpu.make_async_copy(ref, got_x.at[k], kept.at[k]) for k, ref in enumerate((x_own, x_up, x_down))]
    loads += [pltpu.make_async_copy(ref, got_z.at[k], kept.at[4 + k]) for k, ref in enumerate((z_own, z_up, z_down))]
    loads.append(pltpu.make_async_copy(items.at[:, core], got_i.at[0], kept.at[8]))
    for copy in loads:
        copy.start()

    def send(k, src, dst, peer):
        copy = pltpu.make_async_remote_copy(src, dst, sent.at[k], came.at[k], device_id=peer)
        copy.start()
        return copy

    def add_up(parts, to):
        @pl.loop(0, to.shape[0])
        def _(i):
            total = parts[0][i].astype(jnp.float32)
            for part in parts[1:]:
                total += part[i].astype(jnp.float32)
            to[i] = total.astype(to.dtype)

    entered()
    pair = send(0, items.at[:, 1 - core], got_i.at[1], {CORE: 1 - core})
    stages = {
        X: (got_z, 3, sum_z, last_z, 4),
        Z: (got_x, 3, sum_x, last_x, 1),
        Y: (got_i, 2, sum_i, last_i, 7),
    }
    last = {axis: [] for axis in stages}

    def pass_on(axis, s):
        got, parts, total, final, base = stages[axis]
        goal = ahead(axis, s)
        add_up([got.at[j, goal] for j in range(parts)], total.at[s - 1])
        last[axis].append(send(base + s - 1, total.at[s - 1], final.at[s - 1], {axis: goal}))

    for copy in loads[:-1]:
        copy.wait()
    pass_on(Z, 2)
    pass_on(X, 2)
    loads[-1].wait()
    pair.wait()
    for s in (2, 1, 3):
        pass_on(Y, s)
    for s in (1, 3):
        pass_on(Z, s)
        pass_on(X, s)

    for k, axis in enumerate((X, Z)):
        for s in steps:
            pl.semaphore_signal(ready.at[k], inc=1, device_id={axis: ahead(axis, s)})
        pl.semaphore_wait(ready.at[k], 3)

    def ask(group):
        for s in group:
            pltpu.make_async_remote_copy(
                request.at[other(s)], asked.at[me], ask_sent, ask_came, device_id=coords(other(s))
            ).start()

    to_others(ask)
    own_ask = pltpu.make_async_copy(request.at[me], asked.at[me], kept.at[9])
    own_ask.start()
    own_ask.wait()
    rest = pl.ds(0, devices - 1)
    pltpu.make_async_copy(request.at[rest], asked.at[rest], ask_came).wait()
    pltpu.make_async_copy(request.at[rest], asked.at[rest], ask_sent).wait()
    listed = pltpu.make_async_copy(asked, wanted, kept.at[10])
    listed.start()

    def finish(emb, to, start, parts):
        @pl.loop(0, parts[0].shape[0])
        def _(i):
            total = parts[0][i].astype(jnp.float32)
            for part in parts[1:]:
                total += part[i].astype(jnp.float32)
            rows = pl.ds(pl.multiple_of(start + i * tile, tile), tile)
            to[rows] = (emb[rows] + total) * 0.5

    for axis, mine, emb, to, start in (
        (Y, y, item_emb, item_out, 0),
        (Z, z, user_emb, user_out, 0),
        (X, x, user_emb, user_out, half * tile),
    ):
        got, parts, _, final, _ = stages[axis]
        for copy in last[axis]:
            copy.wait()
        finish(emb, to, start, [got.at[j, mine] for j in range(parts)] + [final.at[j] for j in range(3)])
    listed.wait()

    for k in range(each):
        for g in range(stage.shape[0]):
            stage[g, pl.ds(2 * each + k, 1)] = item_out[pl.ds(negatives[k], 1)]

    def pack(goals):
        for g, d in enumerate(goals):
            for k in range(each):
                stage[g, pl.ds(k, 1)] = user_out[pl.ds(wanted[d, 0, k], 1)]
                stage[g, pl.ds(each + k, 1)] = item_out[pl.ds(wanted[d, 0, each + k], 1)]
        for g, d in enumerate(goals):
            packs[d] = stage[g].astype(jnp.bfloat16)

    def give(group):
        goals = [other(s) for s in group]
        pack(goals)
        for d in goals:
            pltpu.make_async_remote_copy(
                packs.at[d], arrived.at[me], row_sent, row_came, device_id=coords(d)
            ).start()

    to_others(give)
    pack([me])
    mine = pltpu.make_async_copy(packs.at[me], arrived.at[me], kept.at[11])
    mine.start()
    mine.wait()
    pltpu.make_async_copy(packs.at[rest], arrived.at[rest], row_came).wait()
    pltpu.make_async_copy(packs.at[rest], arrived.at[rest], row_sent).wait()

    def picked(slot, first):
        rows = arrived[:, pl.ds(first, each)].reshape(devices * each, -1)
        hits = lax.broadcasted_iota(jnp.int32, (slot.shape[0], devices * each), 1) == slot[...]
        return jnp.dot(hits.astype(jnp.bfloat16), rows, preferred_element_type=jnp.float32)

    users = picked(user_slot, 0)
    chosen = picked(item_slot, each)
    positive = jnp.sum(users * chosen, axis=1, keepdims=True)
    against = arrived[:, pl.ds(2 * each, each)].reshape(devices * each, -1)
    margin[...] = (
        lax.dot_general(
            users.astype(jnp.bfloat16), against, (((1,), (1,)), ((), ())),
            preferred_element_type=jnp.float32,
        )
        - positive
    )


def settle(over_x, over_z, items, user_emb, item_emb, request, user_slot, item_slot, negatives):
    side = items.shape[1:]
    embed = user_emb.shape[1]
    half, shard = over_x[0].shape[1], item_emb.shape[0] // side[0]
    items = items.reshape(SIDE, 2, shard, *side)
    devices, each, pairs = request.shape[0], negatives.shape[0], user_slot.shape[0]
    many, one, low = (SIDE, half, *side), (half, *side), jnp.bfloat16
    return pl.pallas_call(
        functools.partial(settle_kernel, devices, each),
        name="settle",
        out_shape=(
            jax.ShapeDtypeStruct(user_emb.shape, jnp.float32),
            jax.ShapeDtypeStruct(item_emb.shape, jnp.float32),
            jax.ShapeDtypeStruct((pairs, devices * each), jnp.float32),
        ),
        in_specs=[ANY] * 7 + [VMEM] * 5 + [SMEM],
        out_specs=(VMEM,) * 3,
        scratch_shapes=[
            pltpu.VMEM((3, *many), low), pltpu.VMEM((3, *many), low),
            pltpu.VMEM((3, *one), low), pltpu.VMEM((3, *one), low),
            pltpu.VMEM((3, *one), low), pltpu.VMEM((3, *one), low),
            pltpu.VMEM((2, SIDE, shard, *side), low), pltpu.VMEM((3, shard, *side), low),
            pltpu.VMEM((3, shard, *side), low),
            pltpu.VMEM((devices, 1, 128), jnp.int32), pltpu.SMEM((devices, 1, 128), jnp.int32),
            pltpu.VMEM((8, 3 * each, embed), jnp.float32),
            pltpu.VMEM((devices, 3 * each, embed), low), pltpu.VMEM((devices, 3 * each, embed), low),
            DMA((10,)), DMA((10,)), DMA((12,)), pltpu.SemaphoreType.REGULAR((2,)), DMA, DMA, DMA, DMA,
        ],
        compiler_params=pltpu.CompilerParams(
            collective_id=1, has_side_effects=True, vmem_limit_bytes=58 * 2**20
        ),
    )(*over_x, *over_z, items, user_emb, item_emb, request, user_slot, item_slot, negatives)


def joined_kernel(*refs):
    for part, came, out in zip(refs[:4], refs[4:8], refs[8:]):
        for i in range(part.shape[1]):
            out[0, i] = (part[0, i].astype(jnp.float32) + came[0, i].astype(jnp.float32)).astype(out.dtype)


def joined(parts, relayed):
    block = (1, *parts[0].shape[1:])
    starts = (0, parts[0].shape[0] // 2) * 2
    spots = [pl.BlockSpec(block, lambda i, start=start: (start + i, 0, 0, 0)) for start in starts]
    return pl.pallas_call(
        joined_kernel,
        name="joined",
        grid=(parts[0].shape[0] // 2,),
        out_shape=[jax.ShapeDtypeStruct(part.shape, part.dtype) for part in parts],
        in_specs=spots + [pl.BlockSpec(block, lambda i: (i, 0, 0, 0))] * 4,
        out_specs=spots,
        input_output_aliases={k: k for k in range(4)},
        compiler_params=pltpu.CompilerParams(vmem_limit_bytes=58 * 2**20),
        cost_estimate=pl.CostEstimate(flops=2**20, bytes_accessed=6 * 2**20, transcendentals=0),
    )(*parts, *relayed)


def tile_kernel(width, depth, users, place, pieces, take, count_ref, rows, cols, vals, *refs):
    parts, outs, (acc, bufs, table, ready, sems, filled, emptied) = refs[:pieces], refs[pieces:-7], refs[-7:]
    total = acc.shape[0] - 1
    count = count_ref[0]
    chunks = (count + width - 1) // width

    def fetch(k, slot):
        return pltpu.make_async_copy(vals.at[pl.ds(k * width, width)], bufs.at[slot], sems.at[slot])

    for k in range(depth - 1):

        @pl.when(k < chunks)
        def _():
            fetch(k, k).start()

    copies = [
        pltpu.make_async_copy(part, table.at[pl.ds(start, part.shape[0])], filled)
        for part, start in place(parts)
    ]
    for copy in copies:
        copy.start()

    @pl.loop(0, total + 1)
    def _(i):
        acc[i] = jnp.zeros(acc.shape[1:], jnp.float32)

    pltpu.make_async_copy(table, table, filled).wait()

    @pl.loop(0, chunks)
    def _(k):
        slot = lax.rem(k, depth)
        ahead = k + depth - 1

        @pl.when(ahead < chunks)
        def _():
            fetch(ahead, lax.rem(ahead, depth)).start()

        fetch(k, slot).wait()
        products = []
        for t in range(width):
            spot = k * width + t
            tile = bufs[slot, t]
            if users:
                left, right, goal = tile, table[cols[spot]], rows[spot]
            else:
                left, right, goal = table[rows[spot]], tile, cols[spot]
            product = jnp.dot(left, right, preferred_element_type=jnp.float32)
            products.append((jnp.where(spot < count, goal, total), product))
        for goal, product in products:
            acc[goal] += product

    for out, start in take(outs):
        rows = pl.ds(start, out.shape[0])

        @pl.loop(0, out.shape[0])
        def _(i, start=start):
            tile = acc[start + i]
            ready[start + i] = (tile if users else tile.T).astype(jnp.bfloat16)

        pltpu.make_async_copy(ready.at[rows], out, emptied).start()
    pltpu.make_async_copy(ready, ready, emptied).wait()


def tile_terms(users, vals, rows, cols, count, parts, place, held, out_shapes, take, width=16, depth=3):
    slots, side, embed = *vals.shape[:2], parts[0].shape[-1]
    total = sum(shape[0] * (shape[1] if len(shape) == 4 else 1) for shape in out_shapes)
    return pl.pallas_call(
        functools.partial(tile_kernel, width, depth, users, place, len(parts), take),
        name="user_terms" if users else "item_terms",
        out_shape=[jax.ShapeDtypeStruct(shape, jnp.bfloat16) for shape in out_shapes],
        in_specs=[SMEM, SMEM, SMEM, ANY] + [ANY] * len(parts),
        out_specs=[ANY] * len(out_shapes),
        scratch_shapes=[
            pltpu.VMEM((total + 1, side, embed), jnp.float32),
            pltpu.VMEM((depth, width, side, side), jnp.bfloat16),
            pltpu.VMEM((held, side, embed), jnp.bfloat16),
            pltpu.VMEM((total, side, embed), jnp.bfloat16),
            DMA((depth,)),
            DMA,
            DMA,
        ],
        compiler_params=pltpu.CompilerParams(vmem_limit_bytes=56 * 2**20),
        cost_estimate=pl.CostEstimate(
            flops=slots * 2 * side * side * embed,
            bytes_accessed=2 * (vals.size + (held + total) * side * embed),
            transcendentals=0,
        ),
    )(count, rows, cols, vals, *parts)


def on_device(
    user_emb,
    item_emb,
    tile_vals,
    tile_rows,
    tile_cols,
    tile_count,
    pair_users,
    pair_items,
    negatives,
):
    row_count = lax.axis_size(ROW)
    col_count = lax.axis_size(COL)
    user_dev = user_emb.shape[2]
    item_dev = item_emb.shape[2]
    embed = user_emb.shape[3]
    side = tile_vals.shape[-1]
    user_each = user_dev // side
    half = user_each // 2
    slots = (tile_vals[0, 0], tile_rows[0, 0], tile_cols[0, 0], tile_count[0])

    devices = row_count * col_count
    neg_each = negatives.shape[0] // devices
    user_rows, item_rows = user_emb.reshape(-1, embed), item_emb.reshape(-1, embed)
    item_tiles, from_x, from_z, user_slot, item_slot, request = first_gather(
        item_rows, user_rows, side, pair_users[None], pair_items[None], (user_dev, item_dev), devices
    )
    near = [(shifted(array, axis, step), 1 if step == 1 else 3, late, 0)
            for step in (1, -1) for array, axis, late in ((from_x, Z, 0), (from_z, X, 1))]

    def item_places(refs):
        return [(refs[0], 0)]

    def item_takes(refs):
        for start in range(0, item_tiles.shape[0], 16):
            yield refs[0].at[pl.ds(start, 16)], start

    def dealt(refs):
        for late, axis in ((0, X), (1, Z)):
            own, up, down, low, high = refs[5 * late : 5 * late + 5]
            for step, to in ((0, own), (1, up), (3, down), (2, None)):
                goal = ahead(axis, step)
                for i in range(SIDE):
                    holder = i * SIDE + goal if late else goal * SIDE + i
                    ref = (low if i < 2 else high).at[i % 2] if to is None else to.at[i]
                    yield ref, holder * user_each + late * half

    many, few = (SIDE, half, side, embed), (SIDE // 2, half, side, embed)
    user_parts = tile_terms(
        True, *slots, [item_tiles], item_places, item_tiles.shape[0],
        [many, many, many, few, few] * 2, dealt,
    )
    relay = []
    for late, axis in ((0, X), (1, Z)):
        for k, step in ((3, 1), (4, -1)):
            relay.append(shifted(user_parts[5 * late + k], axis, step))
    far = []
    for array, back, late, _ in near:
        cut = slice(0, SIDE // 2) if back == 1 else slice(SIDE // 2, SIDE)
        sent_on = shifted(array[cut], X if late else Z, 1 if back == 1 else -1)
        far.append((sent_on, 2, late, cut.start))
    onward = joined([user_parts[k] for k in (1, 2, 6, 7)], relay)
    over_x, over_z = [user_parts[0]], [user_parts[5]]
    for k, (over, axis, step) in enumerate(((over_x, X, 1), (over_x, X, -1), (over_z, Z, 1), (over_z, Z, -1))):
        over.append(shifted(onward[k], axis, step))
    spread = [(from_x, 0, 0, 0), (from_z, 0, 1, 0)] + near + far

    def user_places(refs):
        for ref, (array, back, late, start) in zip(refs, spread):
            at = lax.rem(lax.axis_index(X if late else Z) + SIDE - back, SIDE)
            for i in range(array.shape[0]):
                holder = at * SIDE + start + i if late else (start + i) * SIDE + at
                yield ref.at[i], holder * user_each + late * half

    (item_part,) = tile_terms(
        False, *slots, [part[0] for part in spread], user_places, user_each * col_count,
        [item_tiles.shape], item_takes,
    )
    offset = (lax.axis_index(COL) * row_count + lax.axis_index(ROW)) * item_dev
    device_rank = lax.axis_index(ROW) * col_count + lax.axis_index(COL)
    mine = lax.dynamic_slice_in_dim(negatives, device_rank * neg_each, neg_each, 0) - offset
    user_final, item_final, margin = settle(
        over_x, over_z, item_part, user_rows, item_rows,
        request, user_slot, item_slot, mine,
    )
    bpr_terms = jnp.log1p(jnp.exp(margin))
    return (user_final.reshape(user_emb.shape), item_final.reshape(item_emb.shape), bpr_terms)


def solution(mesh):
    torus = Mesh(mesh.devices.reshape(4, 2, 4, 4), ("row_0", "row_1", "col_0", "col_1"))

    return jax.shard_map(
        on_device,
        mesh=torus,
        in_specs=(
            P(ROW, COL, None, None),
            P(COL, ROW, None, None),
            P(ROW, COL, None, None, None),
            P(ROW, COL, None),
            P(ROW, COL, None),
            P(ROW, COL),
            P(ROW_COL),
            P(ROW_COL),
            P(),
        ),
        out_specs=(P(ROW, COL, None, None), P(COL, ROW, None, None), P(ROW_COL, None)),
        check_vma=False,
    )
```

time: 322 us -> 216 us (0.67)
  blocking collectives: 97.7 us -> 0 us
  Pallas kernels: 45.5 us -> 111 us
  waiting for transfers between devices: 106 us -> 64.6 us
  between operations: 15 us -> 1.45 us
  local copies, waits for them, and re-layouts: 21.6 us -> 13.3 us
  other arithmetic: 5.81 us -> 1.29 us
    all_gather x1 -> x0, waiting for transfers between devices: 74.5 us -> none  [on_device(): lax.all_gather(user_turned.astype(jnp.bfloat16), COL, axis=0, tiled=True)]
    pallas_call x2 -> x5, Pallas kernels: 45.5 us -> 111 us  [the longest x1 54.8 us: settle(): pl.pallas_call(functools.partial(settle_kernel, devices, each), name='set...]
    ppermute x0 -> x16, waiting for transfers between devices: none -> 64.6 us  [shifted(): lax.ppermute(array, axis, [(i, (i + step) % SIDE) for i in range(SIDE)])]
    all_to_all x2 -> x0, blocking collectives: 63.6 us -> none  [the longest x1 33.2 us: sent_and_summed(): lax.all_to_all(blocks, axis, split_axis=0, concat_axis=0, tiled=True)]
    all_gather x4 -> x0, blocking collectives: 34 us -> none  [gather_in_order(): blocks = lax.all_gather(blocks, axes[k], axis=0, tiled=True)]
    all_to_all x4 -> x0, starting transfers between devices: 26.9 us -> none  [the longest x1 8.63 us: on_device(): lax.all_to_all(user_final[user_wanted].astype(jnp.bfloat16), ROW_COL, spl...]
    ppermute x0 -> x16, starting transfers between devices: none -> 24.1 us  [shifted(): lax.ppermute(array, axis, [(i, (i + step) % SIDE) for i in range(SIDE)])]
    all_to_all x4 -> x0, waiting for transfers between devices: 20.8 us -> none  [the longest x1 9.42 us: on_device(): lax.all_to_all(item_request, ROW_COL, split_axis=0, concat_axis=0, tiled=...]
  transfers between devices with their start and end apart: 6 -> 16, of which waited for: 5 -> 5; matrix products, arithmetic and copies ran while one was open for 6% -> 2% of each run, Pallas kernels for 0% -> 14%
where the time goes in v2:
time: 216 us; the launch traced here: 215 us
  Pallas kernels  111 us (51%)
  waiting for transfers between devices  64.6 us (30%)
  starting transfers between devices  24.1 us (11%)
  local copies, waits for them, and re-layouts  13.3 us (6%)
    ppermute x16, waiting for transfers between devices, shifted(): lax.ppermute(array, axis, [(i, (i + step) % SIDE) for i in range(SIDE)])  64.6 us
    pallas_call x1, Pallas kernels, settle(): pl.pallas_call(functools.partial(settle_kernel, devices, each), name='set...  54.8 us
    pallas_call x2, Pallas kernels, tile_terms(): pl.pallas_call(functools.partial(tile_kernel, width, depth, users, place,...  27.9 us
    pallas_call x1, Pallas kernels, first_gather(): pl.pallas_call(functools.partial(first_gather_kernel, widths), name='firs...  24.8 us
    ppermute x16, starting transfers between devices, shifted(): lax.ppermute(array, axis, [(i, (i + step) % SIDE) for i in range(SIDE)])  24.1 us
    unnamed x34, local copies, waits for them, and re-layouts  6.05 us
  transfers between devices with their start and end apart: 16, of which 5 were waited for; matrix products, arithmetic and copies ran while one was open for 2% of the time, Pallas kernels for 14%

profile of v2, /device:TPU:1, one launch (start us, length us, event | category | flops | bytes accessed | tf_op | source)
XLA Modules:
  0.0 215.4 jit_solution(7846742742914101899)
XLA Ops:
  0.6 24.8 %first_gather.1 = (bf16[64,128,128]{2,1,0:T(8,128)(2,1)}, bf16[4,8,128,128]{3,2,1,0:T(8,128)(2,1)}, bf16[4,8,128,128]{3,2,1,0:T(8,128)(2,1)}, s32[512,1]{1,0:T(8...) custom-call(f32[1024,128]{1,0:T(8,128)} %bitcast.18, f32[2048,128]{1,0:T(8,128)} %bitcast.16, s32[1,512]{1,0:T(1,128)} %bitcast.26, ...), custom_call_target="tpu_custom_call" | custom-call | tf_op jit(solution)/shard_map/first_gather/pallas_call | solution.py:118
  25.4 2.8 %collective-permute-start.10 = (bf16[4,8,128,128]{3,2,1,0:T(8,128)(2,1)}, bf16[4,8,128,128]{3,2,1,0:T(8,128)(2,1)S(1)}, u32[]{:S(2)}, u32[]{:S(2)}) collective-permute-start(bf16[4,8,128,128]{3,2,1,0:T(8,128)(2,1)} %get-tuple-element.41.refs_0_), channel_id=1, source_target_pairs={{0,3},{1,0},{2,1},{3,2},{4,7},{5,4},{6,5},{7,6},{8,11},{9,8},{10,9... | collective-permute-start | bytes 3145736 | tf_op jit(solution)/shard_map/ppermute | solution.py:138
  28.9 11.1 %user_terms.1 = (bf16[4,8,128,128]{3,2,1,0:T(8,128)(2,1)}, bf16[4,8,128,128]{3,2,1,0:T(8,128)(2,1)}, bf16[4,8,128,128]{3,2,1,0:T(8,128)(2,1)}, bf16[2,8,128,128]...) custom-call(s32[1]{0:T(128)} %bitcast.11.count_ref, ...), custom_call_target="tpu_custom_call" | custom-call | flops 2147483648 | bytes 27262976 | tf_op jit(solution)/shard_map/user_terms/pallas_call | solution.py:425
  40.0 5.6 %collective-permute-start = (bf16[2,8,128,128]{3,2,1,0:T(8,128)(2,1)}, bf16[2,8,128,128]{3,2,1,0:T(8,128)(2,1)S(1)}, u32[]{:S(2)}, u32[]{:S(2)}) collective-permute-start(bf16[2,8,128,128]{3,2,1,0:T(8,128)(2,1)} %get-tuple-element.32), channel_id=1, source_target_pairs={{0,4},{4,8},{8,12},{12,0},{1,5},{5,9},{9,13},{13,1},{2,6},{6,10},{... | collective-permute-start | bytes 1572872 | tf_op jit(solution)/shard_map/ppermute | solution.py:138
  45.6 4.4 %collective-permute-start.8 = (bf16[4,8,128,128]{3,2,1,0:T(8,128)(2,1)S(1)}, bf16[4,8,128,128]{3,2,1,0:T(8,128)(2,1)S(1)}, u32[]{:S(2)}, u32[]{:S(2)}) collective-permute-start(bf16[4,8,128,128]{3,2,1,0:T(8,128)(2,1)S(1)} %copy-done.4), channel_id=1, source_target_pairs={{0,1},{1,2},{2,3},{3,0},{4,5},{5,6},{6,7},{7,4},{8,9},{9,10},{10,1... | collective-permute-start | bytes 3145736 | tf_op jit(solution)/shard_map/ppermute | solution.py:138
  50.1 2.6 %collective-permute-done.refs_4_ = bf16[2,8,128,128]{3,2,1,0:T(8,128)(2,1)S(1)} collective-permute-done((bf16[2,8,128,128]{3,2,1,0:T(8,128)(2,1)}, bf16[2,8,128,128]{3,2,1,0:T(8,128)(2,1)S(1)}, u32[]{:S(2)}, u32[]{:S(2)}) %collective-permute-start) | collective-permute-done | bytes 524320 | tf_op jit(solution)/shard_map/ppermute | solution.py:138
  52.6 2.1 collective-permute-start.9
  54.7 30.8 %collective-permute-done.1.refs_5_ = bf16[2,8,128,128]{3,2,1,0:T(8,128)(2,1)S(1)} collective-permute-done((bf16[2,8,128,128]{3,2,1,0:T(8,128)(2,1)}, bf16[2,8,128,128]{3,2,1,0:T(8,128)(2,1)S(1)}, u32[]{:S(2)}, u32[]{:S(2)}) %collective-permute-start.1) | collective-permute-done | bytes 524320 | tf_op jit(solution)/shard_map/ppermute | solution.py:138
  86.3 2.0 collective-permute-start.3
  90.3 1.1 collective-permute-start.12
  92.3 6.6 %collective-permute-done.2.refs_6_ = bf16[2,8,128,128]{3,2,1,0:T(8,128)(2,1)S(1)} collective-permute-done((bf16[2,8,128,128]{3,2,1,0:T(8,128)(2,1)}, bf16[2,8,128,128]{3,2,1,0:T(8,128)(2,1)S(1)}, u32[]{:S(2)}, u32[]{:S(2)}) %collective-permute-start.2) | collective-permute-done | bytes 524320 | tf_op jit(solution)/shard_map/ppermute | solution.py:138
  99.7 3.3 %joined.1 = (bf16[4,8,128,128]{3,2,1,0:T(8,128)(2,1)}, bf16[4,8,128,128]{3,2,1,0:T(8,128)(2,1)}, bf16[4,8,128,128]{3,2,1,0:T(8,128)(2,1)}, bf16[4,8,128,128]{3,2,1,0:T(8,128)(2,1)}) custom-call(bf16[4,8,128,128]{3,2,1,0:T(8,128)(2,1)} %get-tuple-element.28.refs_0_, ...), custom_call_target="tpu_custom_call", output_to_operand_aliasing={{0}: (0, {}), {1}: (1, {}), {2}: (2, {}), {3}: (3, {})} | custom-call | flops 1048576 | bytes 6291456 | tf_op jit(solution)/shard_map/joined/pallas_call | solution.py:346
  103.0 1.5 collective-permute-start.4
  104.6 1.2 collective-permute-start.5
  105.8 3.9 %collective-permute-done.14.refs_8_ = bf16[2,8,128,128]{3,2,1,0:T(8,128)(2,1)S(1)} collective-permute-done((bf16[2,8,128,128]{3,2,1,0:T(8,128)(2,1)}, bf16[2,8,128,128]{3,2,1,0:T(8,128)(2,1)S(1)}, u32[]{:S(2)}, u32[]{:S(2)}) %collective-permute-start.14) | collective-permute-done | bytes 524320 | tf_op jit(solution)/shard_map/ppermute | solution.py:138
  109.7 2.0 collective-permute-start.6
  111.7 1.0 collective-permute-start.7
  114.3 1.3 dynamic-slice_subtract_fusion.negatives
  115.6 20.6 %collective-permute-done.13.refs_7_ = bf16[2,8,128,128]{3,2,1,0:T(8,128)(2,1)} collective-permute-done((bf16[2,8,128,128]{3,2,1,0:T(8,128)(2,1)}, bf16[2,8,128,128]{3,2,1,0:T(8,128)(2,1)}, u32[]{:S(2)}, u32[]{:S(2)}) %collective-permute-start.13) | collective-permute-done | bytes 524320 | tf_op jit(solution)/shard_map/ppermute | solution.py:138
  136.2 16.8 %item_terms.1 = bf16[64,128,128]{2,1,0:T(8,128)(2,1)} custom-call(s32[1]{0:T(128)} %bitcast.12.count_ref, s32[512]{0:T(512)} %bitcast.23, s32[512]{0:T(512)} %bitcast.25, bf16[512,128,128]{2,1,0:T(8,128)(2,1)} %bitcast.14, bf16[4,8,128,128]{3,2,1,0:T(8,128)(2,1)} %get-tuple-element.41.refs_0_, bf16[4,8,128,128]{3,2,1,0:T(8,128)(2,1)} %get-tuple-element.42.refs_1_, ...), custom_call_target="tpu_custom_call" | custom-call | flops 2147483648 | bytes 27262976 | tf_op jit(solution)/shard_map/item_terms/pallas_call | solution.py:425
  153.1 0.9 copy-done.6
  154.7 54.8 %settle.1 = (f32[2048,128]{1,0:T(8,128)}, f32[1024,128]{1,0:T(8,128)}, f32[512,1024]{1,0:T(8,128)}) custom-call(bf16[4,8,128,128]{3,2,1,0:T(8,128)(2,1)} %get-tuple-element.27.x_own, bf16[4,8,128,128]{3,2,1,0:T(8,128)(2,1)} %copy-done.6, bf16[4,8,128,128]{3,2,1,0:T(8,128)(2,1)} %copy-done.7, bf16[4,8,128,128]{3,2,1,0:T(8,128)(2,1)} %get-tuple-element.38.z_own, ...), custom_call_target="tpu_custom_call" | custom-call | tf_op jit(solution)/shard_map/settle/pallas_call | solution.py:309
  209.5 3.8 %exponential_log-plus-one_fusion = f32[512,1024]{1,0:T(8,128)} fusion(f32[512,1024]{1,0:T(8,128)} %get-tuple-element.48), kind=kLoop, calls=%fused_computation | loop fusion | bytes 4194304 | tf_op jit(solution)/shard_map/log1p | solution.py:534
  213.2 1.0 copy.23
  (53 shorter events, 8.0 us)
Async XLA Ops:
  25.4 60.1 %collective-permute-start.10 = (bf16[4,8,128,128]{3,2,1,0:T(8,128)(2,1)}, bf16[4,8,128,128]{3,2,1,0:T(8,128)(2,1)S(1)}, u32[]{:S(2)}, u32[]{:S(2)}) collective-permute-start(bf16[4,8,128,128]{3,2,1,0:T(8,128)(2,1)} %get-tuple-element.41.refs_0_), channel_id=1, source_target_pairs={{0,3},{1,0},{2,1},{3,2},{4,7},{5,4},{6,5},{7,6},{8,11},{9,8},{10,9... | collective-permute-start | bytes 3145736 | tf_op jit(solution)/shard_map/ppermute | solution.py:138
  28.9 16.8 %copy-start.4 = (bf16[4,8,128,128]{3,2,1,0:T(8,128)(2,1)S(1)}, bf16[4,8,128,128]{3,2,1,0:T(8,128)(2,1)}, u32[]{:S(2)}) copy-start(bf16[4,8,128,128]{3,2,1,0:T(8,128)(2,1)} %get-tuple-element.41.refs_0_) | copy-start | bytes 3145732
  40.0 12.7 %collective-permute-start = (bf16[2,8,128,128]{3,2,1,0:T(8,128)(2,1)}, bf16[2,8,128,128]{3,2,1,0:T(8,128)(2,1)S(1)}, u32[]{:S(2)}, u32[]{:S(2)}) collective-permute-start(bf16[2,8,128,128]{3,2,1,0:T(8,128)(2,1)} %get-tuple-element.32), channel_id=1, source_target_pairs={{0,4},{4,8},{8,12},{12,0},{1,5},{5,9},{9,13},{13,1},{2,6},{6,10},{... | collective-permute-start | bytes 1572872 | tf_op jit(solution)/shard_map/ppermute | solution.py:138
  45.6 43.5 %collective-permute-start.8 = (bf16[4,8,128,128]{3,2,1,0:T(8,128)(2,1)S(1)}, bf16[4,8,128,128]{3,2,1,0:T(8,128)(2,1)S(1)}, u32[]{:S(2)}, u32[]{:S(2)}) collective-permute-start(bf16[4,8,128,128]{3,2,1,0:T(8,128)(2,1)S(1)} %copy-done.4), channel_id=1, source_target_pairs={{0,1},{1,2},{2,3},{3,0},{4,5},{5,6},{6,7},{7,4},{8,9},{9,10},{10,1... | collective-permute-start | bytes 3145736 | tf_op jit(solution)/shard_map/ppermute | solution.py:138
  50.0 40.3 %collective-permute-start.11 = (bf16[4,8,128,128]{3,2,1,0:T(8,128)(2,1)}, bf16[4,8,128,128]{3,2,1,0:T(8,128)(2,1)S(1)}, u32[]{:S(2)}, u32[]{:S(2)}) collective-permute-start(bf16[4,8,128,128]{3,2,1,0:T(8,128)(2,1)} %get-tuple-element.42.refs_1_), channel_id=1, source_target_pairs={{0,12},{4,0},{8,4},{12,8},{1,13},{5,1},{9,5},{13,9},{2,14},{6,2},{... | collective-permute-start | bytes 3145736 | tf_op jit(solution)/shard_map/ppermute | solution.py:138
  50.0 35.5 %collective-permute-start.1 = (bf16[2,8,128,128]{3,2,1,0:T(8,128)(2,1)}, bf16[2,8,128,128]{3,2,1,0:T(8,128)(2,1)S(1)}, u32[]{:S(2)}, u32[]{:S(2)}) collective-permute-start(bf16[2,8,128,128]{3,2,1,0:T(8,128)(2,1)} %get-tuple-element.33), channel_id=1, source_target_pairs={{0,12},{4,0},{8,4},{12,8},{1,13},{5,1},{9,5},{13,9},{2,14},{6,2},{... | collective-permute-start | bytes 1572872 | tf_op jit(solution)/shard_map/ppermute | solution.py:138
  52.6 39.6 %copy-start.12 = (bf16[2,8,128,128]{3,2,1,0:T(8,128)(2,1)}, bf16[2,8,128,128]{3,2,1,0:T(8,128)(2,1)S(1)}, u32[]{:S(2)}) copy-start(bf16[2,8,128,128]{3,2,1,0:T(8,128)(2,1)S(1)} %collective-permute-done.refs_4_) | copy-start | bytes 1572868
  52.6 51.9 %collective-permute-start.9 = (bf16[4,8,128,128]{3,2,1,0:T(8,128)(2,1)}, bf16[4,8,128,128]{3,2,1,0:T(8,128)(2,1)S(1)}, u32[]{:S(2)}, u32[]{:S(2)}) collective-permute-start(bf16[4,8,128,128]{3,2,1,0:T(8,128)(2,1)} %get-tuple-element.42.refs_1_), channel_id=1, source_target_pairs={{0,4},{4,8},{8,12},{12,0},{1,5},{5,9},{9,13},{13,1},{2,6},{6,10},{... | collective-permute-start | bytes 3145736 | tf_op jit(solution)/shard_map/ppermute | solution.py:138
  85.5 13.4 %collective-permute-start.2 = (bf16[2,8,128,128]{3,2,1,0:T(8,128)(2,1)}, bf16[2,8,128,128]{3,2,1,0:T(8,128)(2,1)S(1)}, u32[]{:S(2)}, u32[]{:S(2)}) collective-permute-start(bf16[2,8,128,128]{3,2,1,0:T(8,128)(2,1)} %get-tuple-element.34), channel_id=1, source_target_pairs={{0,1},{1,2},{2,3},{3,0},{4,5},{5,6},{6,7},{7,4},{8,9},{9,10},{10,1... | collective-permute-start | bytes 1572872 | tf_op jit(solution)/shard_map/ppermute | solution.py:138
  86.3 16.7 %copy-start = (bf16[4,8,128,128]{3,2,1,0:T(8,128)(2,1)}, bf16[4,8,128,128]{3,2,1,0:T(8,128)(2,1)S(1)}, u32[]{:S(2)}) copy-start(bf16[4,8,128,128]{3,2,1,0:T(8,128)(2,1)S(1)} %collective-permute-done.10.refs_4_) | copy-start | bytes 3145732
  86.3 13.4 %collective-permute-start.3 = (bf16[2,8,128,128]{3,2,1,0:T(8,128)(2,1)}, bf16[2,8,128,128]{3,2,1,0:T(8,128)(2,1)}, u32[]{:S(2)}, u32[]{:S(2)}) collective-permute-start(bf16[2,8,128,128]{3,2,1,0:T(8,128)(2,1)} %get-tuple-element.35), channel_id=1, source_target_pairs={{0,3},{1,0},{2,1},{3,2},{4,7},{5,4},{6,5},{7,6},{8,11},{9,8},{10,9... | collective-permute-start | bytes 1572872 | tf_op jit(solution)/shard_map/ppermute | solution.py:138
  89.1 13.9 %copy-start.1 = (bf16[4,8,128,128]{3,2,1,0:T(8,128)(2,1)}, bf16[4,8,128,128]{3,2,1,0:T(8,128)(2,1)S(1)}, u32[]{:S(2)}) copy-start(bf16[4,8,128,128]{3,2,1,0:T(8,128)(2,1)S(1)} %collective-permute-done.8.refs_2_) | copy-start | bytes 3145732
  89.1 20.6 %collective-permute-start.14 = (bf16[2,8,128,128]{3,2,1,0:T(8,128)(2,1)}, bf16[2,8,128,128]{3,2,1,0:T(8,128)(2,1)S(1)}, u32[]{:S(2)}, u32[]{:S(2)}) collective-permute-start(bf16[2,8,128,128]{3,2,1,0:T(8,128)(2,1)} %slice.18), channel_id=1, source_target_pairs={{0,3},{1,0},{2,1},{3,2},{4,7},{5,4},{6,5},{7,6},{8,11},{9,8},{10,9... | collective-permute-start | bytes 1572872 | tf_op jit(solution)/shard_map/ppermute | solution.py:138
  90.3 12.8 %copy-start.2 = (bf16[4,8,128,128]{3,2,1,0:T(8,128)(2,1)}, bf16[4,8,128,128]{3,2,1,0:T(8,128)(2,1)S(1)}, u32[]{:S(2)}) copy-start(bf16[4,8,128,128]{3,2,1,0:T(8,128)(2,1)S(1)} %collective-permute-done.11.refs_5_) | copy-start | bytes 3145732
  90.3 21.5 %collective-permute-start.12 = (bf16[2,8,128,128]{3,2,1,0:T(8,128)(2,1)}, bf16[2,8,128,128]{3,2,1,0:T(8,128)(2,1)S(1)}, u32[]{:S(2)}, u32[]{:S(2)}) collective-permute-start(bf16[2,8,128,128]{3,2,1,0:T(8,128)(2,1)} %slice.16), channel_id=1, source_target_pairs={{0,1},{1,2},{2,3},{3,0},{4,5},{5,6},{6,7},{7,4},{8,9},{9,10},{10,1... | collective-permute-start | bytes 1572872 | tf_op jit(solution)/shard_map/ppermute | solution.py:138
  99.7 13.9 %collective-permute-start.15 = (bf16[2,8,128,128]{3,2,1,0:T(8,128)(2,1)}, bf16[2,8,128,128]{3,2,1,0:T(8,128)(2,1)S(1)}, u32[]{:S(2)}, u32[]{:S(2)}) collective-permute-start(bf16[2,8,128,128]{3,2,1,0:T(8,128)(2,1)} %slice.19), channel_id=1, source_target_pairs={{0,12},{4,0},{8,4},{12,8},{1,13},{5,1},{9,5},{13,9},{2,14},{6,2},{... | collective-permute-start | bytes 1572872 | tf_op jit(solution)/shard_map/ppermute | solution.py:138
  103.0 50.0 %collective-permute-start.4 = (bf16[4,8,128,128]{3,2,1,0:T(8,128)(2,1)}, bf16[4,8,128,128]{3,2,1,0:T(8,128)(2,1)S(1)}, u32[]{:S(2)}, u32[]{:S(2)}) collective-permute-start(bf16[4,8,128,128]{3,2,1,0:T(8,128)(2,1)} %get-tuple-element.36), channel_id=1, source_target_pairs={{0,4},{4,8},{8,12},{12,0},{1,5},{5,9},{9,13},{13,1},{2,6},{6,10},{... | collective-permute-start | bytes 3145736 | tf_op jit(solution)/shard_map/ppermute | solution.py:138
  104.6 8.1 %copy-start.3 = (bf16[4,8,128,128]{3,2,1,0:T(8,128)(2,1)}, bf16[4,8,128,128]{3,2,1,0:T(8,128)(2,1)S(1)}, u32[]{:S(2)}) copy-start(bf16[4,8,128,128]{3,2,1,0:T(8,128)(2,1)S(1)} %collective-permute-done.9.refs_3_) | copy-start | bytes 3145732
  104.6 48.5 %collective-permute-start.5 = (bf16[4,8,128,128]{3,2,1,0:T(8,128)(2,1)}, bf16[4,8,128,128]{3,2,1,0:T(8,128)(2,1)S(1)}, u32[]{:S(2)}, u32[]{:S(2)}) collective-permute-start(bf16[4,8,128,128]{3,2,1,0:T(8,128)(2,1)} %get-tuple-element.37), channel_id=1, source_target_pairs={{0,12},{4,0},{8,4},{12,8},{1,13},{5,1},{9,5},{13,9},{2,14},{6,2},{... | collective-permute-start | bytes 3145736 | tf_op jit(solution)/shard_map/ppermute | solution.py:138
  109.7 3.8 %copy-start.9 = (bf16[2,8,128,128]{3,2,1,0:T(8,128)(2,1)}, bf16[2,8,128,128]{3,2,1,0:T(8,128)(2,1)S(1)}, u32[]{:S(2)}) copy-start(bf16[2,8,128,128]{3,2,1,0:T(8,128)(2,1)S(1)} %collective-permute-done.14.refs_8_) | copy-start | bytes 1572868
  109.7 43.3 %collective-permute-start.6 = (bf16[4,8,128,128]{3,2,1,0:T(8,128)(2,1)}, bf16[4,8,128,128]{3,2,1,0:T(8,128)(2,1)S(1)}, u32[]{:S(2)}, u32[]{:S(2)}) collective-permute-start(bf16[4,8,128,128]{3,2,1,0:T(8,128)(2,1)} %get-tuple-element.39), channel_id=1, source_target_pairs={{0,1},{1,2},{2,3},{3,0},{4,5},{5,6},{6,7},{7,4},{8,9},{9,10},{10,1... | collective-permute-start | bytes 3145736 | tf_op jit(solution)/shard_map/ppermute | solution.py:138
  111.7 41.3 %collective-permute-start.7 = (bf16[4,8,128,128]{3,2,1,0:T(8,128)(2,1)}, bf16[4,8,128,128]{3,2,1,0:T(8,128)(2,1)}, u32[]{:S(2)}, u32[]{:S(2)}) collective-permute-start(bf16[4,8,128,128]{3,2,1,0:T(8,128)(2,1)} %get-tuple-element.40), channel_id=1, source_target_pairs={{0,3},{1,0},{2,1},{3,2},{4,7},{5,4},{6,5},{7,6},{8,11},{9,8},{10,9... | collective-permute-start | bytes 3145736 | tf_op jit(solution)/shard_map/ppermute | solution.py:138
  113.6 22.7 %collective-permute-start.13 = (bf16[2,8,128,128]{3,2,1,0:T(8,128)(2,1)}, bf16[2,8,128,128]{3,2,1,0:T(8,128)(2,1)}, u32[]{:S(2)}, u32[]{:S(2)}) collective-permute-start(bf16[2,8,128,128]{3,2,1,0:T(8,128)(2,1)} %slice.17), channel_id=1, source_target_pairs={{0,4},{4,8},{8,12},{12,0},{1,5},{5,9},{9,13},{13,1},{2,6},{6,10},{... | collective-permute-start | bytes 1572872 | tf_op jit(solution)/shard_map/ppermute | solution.py:138
  209.5 3.8 %copy-start.5 = (f32[2048,128]{1,0:T(8,128)S(1)}, f32[2048,128]{1,0:T(8,128)}, u32[]{:S(2)}) copy-start(f32[2048,128]{1,0:T(8,128)} %get-tuple-element.46) | copy-start | bytes 3145732
  (8 other events, 9.5 us)

commit v3 on v2

--- a/solution.py
+++ b/solution.py
@@ -74,12 +74,16 @@
         copy.start()
         return copy
 
-    copies = []
-    to_y = [send(s - 1, items, place(y, core), {Y: ahead(Y, s)}) for s in steps]
-    copies.append(send(3, items, place(y, core), other))
-    for s in steps:
-        copies.append(send(6 + s, users.at[pl.ds(0, half)], x_out.at[x], {X: ahead(X, s)}))
-        copies.append(send(9 + s, users.at[pl.ds(half, half)], z_out.at[z], {Z: ahead(Z, s)}))
+    ways = {
+        Y: (items, lambda i: place(i, core), 0),
+        X: (users.at[pl.ds(0, half)], lambda i: x_out.at[i], 4),
+        Z: (users.at[pl.ds(half, half)], lambda i: z_out.at[i], 8),
+    }
+    near = {}
+    for axis, (src, spot, base) in ways.items():
+        mine = spot(lax.axis_index(axis))
+        near[axis] = [send(base + k, src, mine, {axis: ahead(axis, s)}) for k, s in enumerate((1, 3))]
+    copies = [send(12, items, place(y, core), other)]
     local = [
         pltpu.make_async_copy(items, place(y, core), kept.at[0]),
         pltpu.make_async_copy(users.at[pl.ds(0, half)], x_out.at[x], kept.at[1]),
@@ -102,10 +106,21 @@
     def _(d):
         request[d] = table[pl.ds(d, 1)]
 
-    for s in steps:
-        to_y[s - 1].wait()
-        back = lax.rem(y + SIDE - s, SIDE)
-        copies.append(send(3 + s, place(back, core), place(back, core), other))
+    far = []
+    for axis, (_, spot, base) in ways.items():
+        for k, s in enumerate((1, 3)):
+            near[axis][k].wait()
+            came_in = spot(ahead(axis, SIDE - s))
+            part = came_in.shape[0] // 2
+            part = came_in.at[pl.ds(k * part, part)]
+            far.append(send(base + 2 + k, part, part, {axis: ahead(axis, s)}))
+            if axis == Y:
+                copies.append(send(13 + k, came_in, came_in, other))
+    for k in range(2):
+        far[k].wait()
+        part = place(ahead(Y, 2), core).at[pl.ds(k * (shard // 2), shard // 2)]
+        copies.append(send(15 + k, part, part, other))
+    copies += far[2:]
     for copy in copies + local:
         copy.wait()
 
@@ -126,7 +141,7 @@
         out_specs=(ANY, ANY, ANY, VMEM, VMEM, VMEM),
         scratch_shapes=[
             pltpu.VMEM((shard, *side), jnp.bfloat16), pltpu.VMEM((2 * half, *side), jnp.bfloat16),
-            pltpu.VMEM((devices, 128), jnp.int32), DMA((13,)), DMA((13,)), DMA((3,)),
+            pltpu.VMEM((devices, 128), jnp.int32), DMA((17,)), DMA((17,)), DMA((3,)),
         ],
         compiler_params=pltpu.CompilerParams(
             collective_id=0, has_side_effects=True, vmem_limit_bytes=58 * 2**20
@@ -146,7 +161,7 @@
     devices, each,
     x_own, x_up, x_down, z_own, z_up, z_down, items, user_emb, item_emb, request, user_slot, item_slot, negatives,
     user_out, item_out, margin,
-    got_x, got_z, sum_x, sum_z, last_x, last_z, got_i, sum_i, last_i, asked, wanted, stage, packs, arrived,
+    got_x, got_z, sum_x, sum_z, last_x, last_z, got_i, sum_i, last_i, asked, wanted, stage, packs, arrived, chosen_negs,
     sent, came, kept, ready, ask_sent, ask_came, row_sent, row_came,
 ):
     y, core, x, z = (lax.axis_index(a) for a in (Y, CORE, X, Z))
@@ -186,7 +201,10 @@
             to[i] = total.astype(to.dtype)
 
     entered()
-    pair = send(0, items.at[:, 1 - core], got_i.at[1], {CORE: 1 - core})
+    pair = {}
+    for s in (2, 1, 3, 0):
+        goal = ahead(Y, s)
+        pair[s] = send(23 + s, items.at[goal, 1 - core], got_i.at[1, goal], {CORE: 1 - core})
     stages = {
         X: (got_z, 3, sum_z, last_z, 4),
         Z: (got_x, 3, sum_x, last_x, 1),
@@ -202,15 +220,14 @@
 
     for copy in loads[:-1]:
         copy.wait()
-    pass_on(Z, 2)
-    pass_on(X, 2)
-    loads[-1].wait()
-    pair.wait()
     for s in (2, 1, 3):
-        pass_on(Y, s)
-    for s in (1, 3):
         pass_on(Z, s)
         pass_on(X, s)
+        if s == 2:
+            loads[-1].wait()
+        pair[s].wait()
+        pass_on(Y, s)
+    pair[0].wait()
 
     for k, axis in enumerate((X, Z)):
         for s in steps:
@@ -242,20 +259,26 @@
             rows = pl.ds(pl.multiple_of(start + i * tile, tile), tile)
             to[rows] = (emb[rows] + total) * 0.5
 
-    for axis, mine, emb, to, start in (
-        (Y, y, item_emb, item_out, 0),
-        (Z, z, user_emb, user_out, 0),
-        (X, x, user_emb, user_out, half * tile),
-    ):
+    def settle_axis(axis, mine, emb, to, start):
         got, parts, _, final, _ = stages[axis]
         for copy in last[axis]:
             copy.wait()
         finish(emb, to, start, [got.at[j, mine] for j in range(parts)] + [final.at[j] for j in range(3)])
+
+    settle_axis(Y, y, item_emb, item_out, 0)
+    for k in range(each):
+        stage[0, pl.ds(k, 1)] = item_out[pl.ds(negatives[k], 1)]
+    group = y * 2 + core
+    chosen_negs[group, x, z] = stage[0, pl.ds(0, each)].astype(jnp.bfloat16)
+    own = chosen_negs.at[group, x, z]
+    first = [send(9 + s, own, own, {X: ahead(X, s)}) for s in steps]
+    settle_axis(Z, z, user_emb, user_out, 0)
+    settle_axis(X, x, user_emb, user_out, half * tile)
     listed.wait()
-
-    for k in range(each):
-        for g in range(stage.shape[0]):
-            stage[g, pl.ds(2 * each + k, 1)] = item_out[pl.ds(negatives[k], 1)]
+    for copy in first:
+        copy.wait()
+    line = chosen_negs.at[group, :, z]
+    second = [send(12 + s, line, line, {Z: ahead(Z, s)}) for s in steps]
 
     def pack(goals):
         for g, d in enumerate(goals):
@@ -274,12 +297,18 @@
             ).start()
 
     to_others(give)
+    for copy in second:
+        copy.wait()
+    plane = chosen_negs.at[group]
+    third = [send(16 + k, plane, plane, mate) for k, mate in enumerate(mates)]
     pack([me])
     mine = pltpu.make_async_copy(packs.at[me], arrived.at[me], kept.at[11])
     mine.start()
     mine.wait()
     pltpu.make_async_copy(packs.at[rest], arrived.at[rest], row_came).wait()
     pltpu.make_async_copy(packs.at[rest], arrived.at[rest], row_sent).wait()
+    for copy in third:
+        copy.wait()
 
     def picked(slot, first):
         rows = arrived[:, pl.ds(first, each)].reshape(devices * each, -1)
@@ -289,7 +318,7 @@
     users = picked(user_slot, 0)
     chosen = picked(item_slot, each)
     positive = jnp.sum(users * chosen, axis=1, keepdims=True)
-    against = arrived[:, pl.ds(2 * each, each)].reshape(devices * each, -1)
+    against = chosen_negs[...].reshape(devices * each, -1)
     margin[...] = (
         lax.dot_general(
             users.astype(jnp.bfloat16), against, (((1,), (1,)), ((), ())),
@@ -323,9 +352,10 @@
             pltpu.VMEM((2, SIDE, shard, *side), low), pltpu.VMEM((3, shard, *side), low),
             pltpu.VMEM((3, shard, *side), low),
             pltpu.VMEM((devices, 1, 128), jnp.int32), pltpu.SMEM((devices, 1, 128), jnp.int32),
-            pltpu.VMEM((8, 3 * each, embed), jnp.float32),
-            pltpu.VMEM((devices, 3 * each, embed), low), pltpu.VMEM((devices, 3 * each, embed), low),
-            DMA((10,)), DMA((10,)), DMA((12,)), pltpu.SemaphoreType.REGULAR((2,)), DMA, DMA, DMA, DMA,
+            pltpu.VMEM((8, 2 * each, embed), jnp.float32),
+            pltpu.VMEM((devices, 2 * each, embed), low), pltpu.VMEM((devices, 2 * each, embed), low),
+            pltpu.VMEM((2 * SIDE, SIDE, SIDE, each, embed), low),
+            DMA((27,)), DMA((27,)), DMA((12,)), pltpu.SemaphoreType.REGULAR((2,)), DMA, DMA, DMA, DMA,
         ],
         compiler_params=pltpu.CompilerParams(
             collective_id=1, has_side_effects=True, vmem_limit_bytes=58 * 2**20
@@ -419,7 +449,7 @@
     pltpu.make_async_copy(ready, ready, emptied).wait()
 
 
-def tile_terms(users, vals, rows, cols, count, parts, place, held, out_shapes, take, width=16, depth=3):
+def tile_terms(users, vals, rows, cols, count, parts, place, held, out_shapes, take, width=64, depth=3):
     slots, side, embed = *vals.shape[:2], parts[0].shape[-1]
     total = sum(shape[0] * (shape[1] if len(shape) == 4 else 1) for shape in out_shapes)
     return pl.pallas_call(

time: 216 us -> 202 us (0.935)
  Pallas kernels: 111 us -> 105 us
  waiting for transfers between devices: 64.6 us -> 59.4 us
    ppermute x16, waiting for transfers between devices: 64.6 us -> 59.4 us  [shifted(): lax.ppermute(array, axis, [(i, (i + step) % SIDE) for i in range(SIDE)])]
    pallas_call x2, Pallas kernels: 27.9 us -> 24.3 us  [tile_terms(): pl.pallas_call(functools.partial(tile_kernel, width, depth, users, place,...]
where the time goes in v3:
time: 202 us
  Pallas kernels  105 us (52%)
  waiting for transfers between devices  59.4 us (29%)
  starting transfers between devices  22.7 us (11%)
  local copies, waits for them, and re-layouts  11.7 us (6%)
    ppermute x16, waiting for transfers between devices, shifted(): lax.ppermute(array, axis, [(i, (i + step) % SIDE) for i in range(SIDE)])  59.4 us
    pallas_call x1, Pallas kernels, settle(): pl.pallas_call(functools.partial(settle_kernel, devices, each), name='set...  54.7 us
    pallas_call x2, Pallas kernels, tile_terms(): pl.pallas_call(functools.partial(tile_kernel, width, depth, users, place,...  24.3 us
    ppermute x16, starting transfers between devices, shifted(): lax.ppermute(array, axis, [(i, (i + step) % SIDE) for i in range(SIDE)])  22.7 us
    pallas_call x1, Pallas kernels, first_gather(): pl.pallas_call(functools.partial(first_gather_kernel, widths), name='firs...  22.7 us
    unnamed x34, local copies, waits for them, and re-layouts  4.59 us
  transfers between devices with their start and end apart: 16, of which 5 were waited for; matrix products, arithmetic and copies ran while one was open for 2% of the time, Pallas kernels for 14%

profile of v3, /device:TPU:1, one launch (start us, length us, event | category | flops | bytes accessed | tf_op | source)
XLA Modules:
  0.0 201.6 jit_solution(12650821954243790627)
XLA Ops:
  0.6 22.7 %first_gather.1 = (bf16[64,128,128]{2,1,0:T(8,128)(2,1)}, bf16[4,8,128,128]{3,2,1,0:T(8,128)(2,1)}, bf16[4,8,128,128]{3,2,1,0:T(8,128)(2,1)}, s32[512,1]{1,0:T(8...) custom-call(f32[1024,128]{1,0:T(8,128)} %bitcast.18, f32[2048,128]{1,0:T(8,128)} %bitcast.16, s32[1,512]{1,0:T(1,128)} %bitcast.26, ...), custom_call_target="tpu_custom_call" | custom-call | tf_op jit(solution)/shard_map/first_gather/pallas_call | solution.py:133
  23.3 2.8 %collective-permute-start.10 = (bf16[4,8,128,128]{3,2,1,0:T(8,128)(2,1)}, bf16[4,8,128,128]{3,2,1,0:T(8,128)(2,1)S(1)}, u32[]{:S(2)}, u32[]{:S(2)}) collective-permute-start(bf16[4,8,128,128]{3,2,1,0:T(8,128)(2,1)} %get-tuple-element.41.refs_0_), channel_id=1, source_target_pairs={{0,3},{1,0},{2,1},{3,2},{4,7},{5,4},{6,5},{7,6},{8,11},{9,8},{10,9... | collective-permute-start | bytes 3145736 | tf_op jit(solution)/shard_map/ppermute | solution.py:153
  26.8 9.0 %user_terms.1 = (bf16[4,8,128,128]{3,2,1,0:T(8,128)(2,1)}, bf16[4,8,128,128]{3,2,1,0:T(8,128)(2,1)}, bf16[4,8,128,128]{3,2,1,0:T(8,128)(2,1)}, bf16[2,8,128,128]...) custom-call(s32[1]{0:T(128)} %bitcast.11.count_ref, ...), custom_call_target="tpu_custom_call" | custom-call | flops 2147483648 | bytes 27262976 | tf_op jit(solution)/shard_map/user_terms/pallas_call | solution.py:455
  35.8 3.0 %collective-permute-start = (bf16[2,8,128,128]{3,2,1,0:T(8,128)(2,1)}, bf16[2,8,128,128]{3,2,1,0:T(8,128)(2,1)S(1)}, u32[]{:S(2)}, u32[]{:S(2)}) collective-permute-start(bf16[2,8,128,128]{3,2,1,0:T(8,128)(2,1)} %get-tuple-element.32), channel_id=1, source_target_pairs={{0,4},{4,8},{8,12},{12,0},{1,5},{5,9},{9,13},{13,1},{2,6},{6,10},{... | collective-permute-start | bytes 1572872 | tf_op jit(solution)/shard_map/ppermute | solution.py:153
  38.7 1.4 collective-permute-start.8
  40.1 1.5 collective-permute-start.11
  42.0 6.8 %collective-permute-done.refs_4_ = bf16[2,8,128,128]{3,2,1,0:T(8,128)(2,1)S(1)} collective-permute-done((bf16[2,8,128,128]{3,2,1,0:T(8,128)(2,1)}, bf16[2,8,128,128]{3,2,1,0:T(8,128)(2,1)S(1)}, u32[]{:S(2)}, u32[]{:S(2)}) %collective-permute-start) | collective-permute-done | bytes 524320 | tf_op jit(solution)/shard_map/ppermute | solution.py:153
  48.8 2.1 %collective-permute-start.9 = (bf16[4,8,128,128]{3,2,1,0:T(8,128)(2,1)}, bf16[4,8,128,128]{3,2,1,0:T(8,128)(2,1)S(1)}, u32[]{:S(2)}, u32[]{:S(2)}) collective-permute-start(bf16[4,8,128,128]{3,2,1,0:T(8,128)(2,1)} %get-tuple-element.42.refs_1_), channel_id=1, source_target_pairs={{0,4},{4,8},{8,12},{12,0},{1,5},{5,9},{9,13},{13,1},{2,6},{6,10},{... | collective-permute-start | bytes 3145736 | tf_op jit(solution)/shard_map/ppermute | solution.py:153
  50.9 24.8 %collective-permute-done.1.refs_5_ = bf16[2,8,128,128]{3,2,1,0:T(8,128)(2,1)S(1)} collective-permute-done((bf16[2,8,128,128]{3,2,1,0:T(8,128)(2,1)}, bf16[2,8,128,128]{3,2,1,0:T(8,128)(2,1)S(1)}, u32[]{:S(2)}, u32[]{:S(2)}) %collective-permute-start.1) | collective-permute-done | bytes 524320 | tf_op jit(solution)/shard_map/ppermute | solution.py:153
  76.5 1.9 collective-permute-start.3
  80.6 0.9 collective-permute-start.12
  82.4 6.6 %collective-permute-done.2.refs_6_ = bf16[2,8,128,128]{3,2,1,0:T(8,128)(2,1)S(1)} collective-permute-done((bf16[2,8,128,128]{3,2,1,0:T(8,128)(2,1)}, bf16[2,8,128,128]{3,2,1,0:T(8,128)(2,1)S(1)}, u32[]{:S(2)}, u32[]{:S(2)}) %collective-permute-start.2) | collective-permute-done | bytes 524320 | tf_op jit(solution)/shard_map/ppermute | solution.py:153
  89.8 3.3 %joined.1 = (bf16[4,8,128,128]{3,2,1,0:T(8,128)(2,1)}, bf16[4,8,128,128]{3,2,1,0:T(8,128)(2,1)}, bf16[4,8,128,128]{3,2,1,0:T(8,128)(2,1)}, bf16[4,8,128,128]{3,2,1,0:T(8,128)(2,1)}) custom-call(bf16[4,8,128,128]{3,2,1,0:T(8,128)(2,1)} %get-tuple-element.28.refs_0_, ...), custom_call_target="tpu_custom_call", output_to_operand_aliasing={{0}: (0, {}), {1}: (1, {}), {2}: (2, {}), {3}: (3, {})} | custom-call | flops 1048576 | bytes 6291456 | tf_op jit(solution)/shard_map/joined/pallas_call | solution.py:376
  93.2 1.9 collective-permute-start.4
  95.9 4.2 %collective-permute-done.14.refs_8_ = bf16[2,8,128,128]{3,2,1,0:T(8,128)(2,1)S(1)} collective-permute-done((bf16[2,8,128,128]{3,2,1,0:T(8,128)(2,1)}, bf16[2,8,128,128]{3,2,1,0:T(8,128)(2,1)S(1)}, u32[]{:S(2)}, u32[]{:S(2)}) %collective-permute-start.14) | collective-permute-done | bytes 524320 | tf_op jit(solution)/shard_map/ppermute | solution.py:153
  100.1 2.1 %collective-permute-start.6 = (bf16[4,8,128,128]{3,2,1,0:T(8,128)(2,1)}, bf16[4,8,128,128]{3,2,1,0:T(8,128)(2,1)S(1)}, u32[]{:S(2)}, u32[]{:S(2)}) collective-permute-start(bf16[4,8,128,128]{3,2,1,0:T(8,128)(2,1)} %get-tuple-element.39), channel_id=1, source_target_pairs={{0,1},{1,2},{2,3},{3,0},{4,5},{5,6},{6,7},{7,4},{8,9},{9,10},{10,1... | collective-permute-start | bytes 3145736 | tf_op jit(solution)/shard_map/ppermute | solution.py:153
  103.7 1.9 collective-permute-start.13
  105.6 1.3 dynamic-slice_subtract_fusion.negatives
  106.9 17.0 %collective-permute-done.13.refs_7_ = bf16[2,8,128,128]{3,2,1,0:T(8,128)(2,1)} collective-permute-done((bf16[2,8,128,128]{3,2,1,0:T(8,128)(2,1)}, bf16[2,8,128,128]{3,2,1,0:T(8,128)(2,1)}, u32[]{:S(2)}, u32[]{:S(2)}) %collective-permute-start.13) | collective-permute-done | bytes 524320 | tf_op jit(solution)/shard_map/ppermute | solution.py:153
  123.9 15.3 %item_terms.1 = bf16[64,128,128]{2,1,0:T(8,128)(2,1)} custom-call(s32[1]{0:T(128)} %bitcast.12.count_ref, s32[512]{0:T(512)} %bitcast.23, s32[512]{0:T(512)} %bitcast.25, bf16[512,128,128]{2,1,0:T(8,128)(2,1)} %bitcast.14, bf16[4,8,128,128]{3,2,1,0:T(8,128)(2,1)} %get-tuple-element.41.refs_0_, bf16[4,8,128,128]{3,2,1,0:T(8,128)(2,1)} %get-tuple-element.42.refs_1_, ...), custom_call_target="tpu_custom_call" | custom-call | flops 2147483648 | bytes 27262976 | tf_op jit(solution)/shard_map/item_terms/pallas_call | solution.py:455
  139.3 0.9 copy-done.6
  140.8 54.7 %settle.1 = (f32[2048,128]{1,0:T(8,128)}, f32[1024,128]{1,0:T(8,128)}, f32[512,1024]{1,0:T(8,128)}) custom-call(bf16[4,8,128,128]{3,2,1,0:T(8,128)(2,1)} %get-tuple-element.27.x_own, bf16[4,8,128,128]{3,2,1,0:T(8,128)(2,1)} %copy-done.6, bf16[4,8,128,128]{3,2,1,0:T(8,128)(2,1)} %copy-done.7, bf16[4,8,128,128]{3,2,1,0:T(8,128)(2,1)} %get-tuple-element.38.z_own, ...), custom_call_target="tpu_custom_call" | custom-call | tf_op jit(solution)/shard_map/settle/pallas_call | solution.py:338
  195.6 3.8 %exponential_log-plus-one_fusion = f32[512,1024]{1,0:T(8,128)} fusion(f32[512,1024]{1,0:T(8,128)} %get-tuple-element.48), kind=kLoop, calls=%fused_computation | loop fusion | bytes 4194304 | tf_op jit(solution)/shard_map/log1p | solution.py:564
  199.4 1.0 copy.23
  (53 shorter events, 9.4 us)
Async XLA Ops:
  23.3 53.2 %collective-permute-start.10 = (bf16[4,8,128,128]{3,2,1,0:T(8,128)(2,1)}, bf16[4,8,128,128]{3,2,1,0:T(8,128)(2,1)S(1)}, u32[]{:S(2)}, u32[]{:S(2)}) collective-permute-start(bf16[4,8,128,128]{3,2,1,0:T(8,128)(2,1)} %get-tuple-element.41.refs_0_), channel_id=1, source_target_pairs={{0,3},{1,0},{2,1},{3,2},{4,7},{5,4},{6,5},{7,6},{8,11},{9,8},{10,9... | collective-permute-start | bytes 3145736 | tf_op jit(solution)/shard_map/ppermute | solution.py:153
  26.8 12.0 %copy-start.4 = (bf16[4,8,128,128]{3,2,1,0:T(8,128)(2,1)S(1)}, bf16[4,8,128,128]{3,2,1,0:T(8,128)(2,1)}, u32[]{:S(2)}) copy-start(bf16[4,8,128,128]{3,2,1,0:T(8,128)(2,1)} %get-tuple-element.41.refs_0_) | copy-start | bytes 3145732
  35.8 13.0 %collective-permute-start = (bf16[2,8,128,128]{3,2,1,0:T(8,128)(2,1)}, bf16[2,8,128,128]{3,2,1,0:T(8,128)(2,1)S(1)}, u32[]{:S(2)}, u32[]{:S(2)}) collective-permute-start(bf16[2,8,128,128]{3,2,1,0:T(8,128)(2,1)} %get-tuple-element.32), channel_id=1, source_target_pairs={{0,4},{4,8},{8,12},{12,0},{1,5},{5,9},{9,13},{13,1},{2,6},{6,10},{... | collective-permute-start | bytes 1572872 | tf_op jit(solution)/shard_map/ppermute | solution.py:153
  38.7 40.5 %collective-permute-start.8 = (bf16[4,8,128,128]{3,2,1,0:T(8,128)(2,1)S(1)}, bf16[4,8,128,128]{3,2,1,0:T(8,128)(2,1)S(1)}, u32[]{:S(2)}, u32[]{:S(2)}) collective-permute-start(bf16[4,8,128,128]{3,2,1,0:T(8,128)(2,1)S(1)} %copy-done.4), channel_id=1, source_target_pairs={{0,1},{1,2},{2,3},{3,0},{4,5},{5,6},{6,7},{7,4},{8,9},{9,10},{10,1... | collective-permute-start | bytes 3145736 | tf_op jit(solution)/shard_map/ppermute | solution.py:153
  40.1 40.5 %collective-permute-start.11 = (bf16[4,8,128,128]{3,2,1,0:T(8,128)(2,1)}, bf16[4,8,128,128]{3,2,1,0:T(8,128)(2,1)S(1)}, u32[]{:S(2)}, u32[]{:S(2)}) collective-permute-start(bf16[4,8,128,128]{3,2,1,0:T(8,128)(2,1)} %get-tuple-element.42.refs_1_), channel_id=1, source_target_pairs={{0,12},{4,0},{8,4},{12,8},{1,13},{5,1},{9,5},{13,9},{2,14},{6,2},{... | collective-permute-start | bytes 3145736 | tf_op jit(solution)/shard_map/ppermute | solution.py:153
  41.6 34.1 %collective-permute-start.1 = (bf16[2,8,128,128]{3,2,1,0:T(8,128)(2,1)}, bf16[2,8,128,128]{3,2,1,0:T(8,128)(2,1)S(1)}, u32[]{:S(2)}, u32[]{:S(2)}) collective-permute-start(bf16[2,8,128,128]{3,2,1,0:T(8,128)(2,1)} %get-tuple-element.33), channel_id=1, source_target_pairs={{0,12},{4,0},{8,4},{12,8},{1,13},{5,1},{9,5},{13,9},{2,14},{6,2},{... | collective-permute-start | bytes 1572872 | tf_op jit(solution)/shard_map/ppermute | solution.py:153
  48.8 33.6 %copy-start.12 = (bf16[2,8,128,128]{3,2,1,0:T(8,128)(2,1)}, bf16[2,8,128,128]{3,2,1,0:T(8,128)(2,1)S(1)}, u32[]{:S(2)}) copy-start(bf16[2,8,128,128]{3,2,1,0:T(8,128)(2,1)S(1)} %collective-permute-done.refs_4_) | copy-start | bytes 1572868
  48.8 46.3 %collective-permute-start.9 = (bf16[4,8,128,128]{3,2,1,0:T(8,128)(2,1)}, bf16[4,8,128,128]{3,2,1,0:T(8,128)(2,1)S(1)}, u32[]{:S(2)}, u32[]{:S(2)}) collective-permute-start(bf16[4,8,128,128]{3,2,1,0:T(8,128)(2,1)} %get-tuple-element.42.refs_1_), channel_id=1, source_target_pairs={{0,4},{4,8},{8,12},{12,0},{1,5},{5,9},{9,13},{13,1},{2,6},{6,10},{... | collective-permute-start | bytes 3145736 | tf_op jit(solution)/shard_map/ppermute | solution.py:153
  75.6 13.4 %collective-permute-start.2 = (bf16[2,8,128,128]{3,2,1,0:T(8,128)(2,1)}, bf16[2,8,128,128]{3,2,1,0:T(8,128)(2,1)S(1)}, u32[]{:S(2)}, u32[]{:S(2)}) collective-permute-start(bf16[2,8,128,128]{3,2,1,0:T(8,128)(2,1)} %get-tuple-element.34), channel_id=1, source_target_pairs={{0,1},{1,2},{2,3},{3,0},{4,5},{5,6},{6,7},{7,4},{8,9},{9,10},{10,1... | collective-permute-start | bytes 1572872 | tf_op jit(solution)/shard_map/ppermute | solution.py:153
  76.5 16.7 %copy-start = (bf16[4,8,128,128]{3,2,1,0:T(8,128)(2,1)}, bf16[4,8,128,128]{3,2,1,0:T(8,128)(2,1)S(1)}, u32[]{:S(2)}) copy-start(bf16[4,8,128,128]{3,2,1,0:T(8,128)(2,1)S(1)} %collective-permute-done.10.refs_4_) | copy-start | bytes 3145732
  76.5 13.3 %collective-permute-start.3 = (bf16[2,8,128,128]{3,2,1,0:T(8,128)(2,1)}, bf16[2,8,128,128]{3,2,1,0:T(8,128)(2,1)}, u32[]{:S(2)}, u32[]{:S(2)}) collective-permute-start(bf16[2,8,128,128]{3,2,1,0:T(8,128)(2,1)} %get-tuple-element.35), channel_id=1, source_target_pairs={{0,3},{1,0},{2,1},{3,2},{4,7},{5,4},{6,5},{7,6},{8,11},{9,8},{10,9... | collective-permute-start | bytes 1572872 | tf_op jit(solution)/shard_map/ppermute | solution.py:153
  79.2 13.9 %copy-start.1 = (bf16[4,8,128,128]{3,2,1,0:T(8,128)(2,1)}, bf16[4,8,128,128]{3,2,1,0:T(8,128)(2,1)S(1)}, u32[]{:S(2)}) copy-start(bf16[4,8,128,128]{3,2,1,0:T(8,128)(2,1)S(1)} %collective-permute-done.8.refs_2_) | copy-start | bytes 3145732
  79.2 20.8 %collective-permute-start.14 = (bf16[2,8,128,128]{3,2,1,0:T(8,128)(2,1)}, bf16[2,8,128,128]{3,2,1,0:T(8,128)(2,1)S(1)}, u32[]{:S(2)}, u32[]{:S(2)}) collective-permute-start(bf16[2,8,128,128]{3,2,1,0:T(8,128)(2,1)} %slice.18), channel_id=1, source_target_pairs={{0,3},{1,0},{2,1},{3,2},{4,7},{5,4},{6,5},{7,6},{8,11},{9,8},{10,9... | collective-permute-start | bytes 1572872 | tf_op jit(solution)/shard_map/ppermute | solution.py:153
  80.6 12.5 %copy-start.2 = (bf16[4,8,128,128]{3,2,1,0:T(8,128)(2,1)}, bf16[4,8,128,128]{3,2,1,0:T(8,128)(2,1)S(1)}, u32[]{:S(2)}) copy-start(bf16[4,8,128,128]{3,2,1,0:T(8,128)(2,1)S(1)} %collective-permute-done.11.refs_5_) | copy-start | bytes 3145732
  80.6 21.6 %collective-permute-start.12 = (bf16[2,8,128,128]{3,2,1,0:T(8,128)(2,1)}, bf16[2,8,128,128]{3,2,1,0:T(8,128)(2,1)S(1)}, u32[]{:S(2)}, u32[]{:S(2)}) collective-permute-start(bf16[2,8,128,128]{3,2,1,0:T(8,128)(2,1)} %slice.16), channel_id=1, source_target_pairs={{0,1},{1,2},{2,3},{3,0},{4,5},{5,6},{6,7},{7,4},{8,9},{9,10},{10,1... | collective-permute-start | bytes 1572872 | tf_op jit(solution)/shard_map/ppermute | solution.py:153
  89.8 13.9 %collective-permute-start.15 = (bf16[2,8,128,128]{3,2,1,0:T(8,128)(2,1)}, bf16[2,8,128,128]{3,2,1,0:T(8,128)(2,1)S(1)}, u32[]{:S(2)}, u32[]{:S(2)}) collective-permute-start(bf16[2,8,128,128]{3,2,1,0:T(8,128)(2,1)} %slice.19), channel_id=1, source_target_pairs={{0,12},{4,0},{8,4},{12,8},{1,13},{5,1},{9,5},{13,9},{2,14},{6,2},{... | collective-permute-start | bytes 1572872 | tf_op jit(solution)/shard_map/ppermute | solution.py:153
  93.2 46.0 %collective-permute-start.4 = (bf16[4,8,128,128]{3,2,1,0:T(8,128)(2,1)}, bf16[4,8,128,128]{3,2,1,0:T(8,128)(2,1)S(1)}, u32[]{:S(2)}, u32[]{:S(2)}) collective-permute-start(bf16[4,8,128,128]{3,2,1,0:T(8,128)(2,1)} %get-tuple-element.36), channel_id=1, source_target_pairs={{0,4},{4,8},{8,12},{12,0},{1,5},{5,9},{9,13},{13,1},{2,6},{6,10},{... | collective-permute-start | bytes 3145736 | tf_op jit(solution)/shard_map/ppermute | solution.py:153
  95.0 7.8 %copy-start.3 = (bf16[4,8,128,128]{3,2,1,0:T(8,128)(2,1)}, bf16[4,8,128,128]{3,2,1,0:T(8,128)(2,1)S(1)}, u32[]{:S(2)}) copy-start(bf16[4,8,128,128]{3,2,1,0:T(8,128)(2,1)S(1)} %collective-permute-done.9.refs_3_) | copy-start | bytes 3145732
  95.0 44.2 %collective-permute-start.5 = (bf16[4,8,128,128]{3,2,1,0:T(8,128)(2,1)}, bf16[4,8,128,128]{3,2,1,0:T(8,128)(2,1)S(1)}, u32[]{:S(2)}, u32[]{:S(2)}) collective-permute-start(bf16[4,8,128,128]{3,2,1,0:T(8,128)(2,1)} %get-tuple-element.37), channel_id=1, source_target_pairs={{0,12},{4,0},{8,4},{12,8},{1,13},{5,1},{9,5},{13,9},{2,14},{6,2},{... | collective-permute-start | bytes 3145736 | tf_op jit(solution)/shard_map/ppermute | solution.py:153
  100.1 3.6 %copy-start.9 = (bf16[2,8,128,128]{3,2,1,0:T(8,128)(2,1)}, bf16[2,8,128,128]{3,2,1,0:T(8,128)(2,1)S(1)}, u32[]{:S(2)}) copy-start(bf16[2,8,128,128]{3,2,1,0:T(8,128)(2,1)S(1)} %collective-permute-done.14.refs_8_) | copy-start | bytes 1572868
  100.1 39.2 %collective-permute-start.6 = (bf16[4,8,128,128]{3,2,1,0:T(8,128)(2,1)}, bf16[4,8,128,128]{3,2,1,0:T(8,128)(2,1)S(1)}, u32[]{:S(2)}, u32[]{:S(2)}) collective-permute-start(bf16[4,8,128,128]{3,2,1,0:T(8,128)(2,1)} %get-tuple-element.39), channel_id=1, source_target_pairs={{0,1},{1,2},{2,3},{3,0},{4,5},{5,6},{6,7},{7,4},{8,9},{9,10},{10,1... | collective-permute-start | bytes 3145736 | tf_op jit(solution)/shard_map/ppermute | solution.py:153
  102.2 37.0 %collective-permute-start.7 = (bf16[4,8,128,128]{3,2,1,0:T(8,128)(2,1)}, bf16[4,8,128,128]{3,2,1,0:T(8,128)(2,1)}, u32[]{:S(2)}, u32[]{:S(2)}) collective-permute-start(bf16[4,8,128,128]{3,2,1,0:T(8,128)(2,1)} %get-tuple-element.40), channel_id=1, source_target_pairs={{0,3},{1,0},{2,1},{3,2},{4,7},{5,4},{6,5},{7,6},{8,11},{9,8},{10,9... | collective-permute-start | bytes 3145736 | tf_op jit(solution)/shard_map/ppermute | solution.py:153
  103.7 20.2 %collective-permute-start.13 = (bf16[2,8,128,128]{3,2,1,0:T(8,128)(2,1)}, bf16[2,8,128,128]{3,2,1,0:T(8,128)(2,1)}, u32[]{:S(2)}, u32[]{:S(2)}) collective-permute-start(bf16[2,8,128,128]{3,2,1,0:T(8,128)(2,1)} %slice.17), channel_id=1, source_target_pairs={{0,4},{4,8},{8,12},{12,0},{1,5},{5,9},{9,13},{13,1},{2,6},{6,10},{... | collective-permute-start | bytes 1572872 | tf_op jit(solution)/shard_map/ppermute | solution.py:153
  195.6 3.8 %copy-start.5 = (f32[2048,128]{1,0:T(8,128)S(1)}, f32[2048,128]{1,0:T(8,128)}, u32[]{:S(2)}) copy-start(f32[2048,128]{1,0:T(8,128)} %get-tuple-element.46) | copy-start | bytes 3145732
  (8 other events, 10.3 us)

commit v4 on v3

--- a/solution.py
+++ b/solution.py
@@ -16,6 +16,7 @@
 VMEM = pl.BlockSpec(memory_space=pltpu.VMEM)
 SMEM = pl.BlockSpec(memory_space=pltpu.SMEM)
 DMA = pltpu.SemaphoreType.DMA
+WHOLE = 67_043_328
 ROW_COL = ("row_0", "row_1", "col_0", "col_1")
 
 
@@ -51,19 +52,29 @@
 
 
 def first_gather_kernel(
-    widths, item_emb, user_emb, pair_users, pair_items, items_out, x_out, z_out, user_slot, item_slot, request,
-    items, users, table, sent, came, kept,
+    widths, item_emb, user_emb, pair_users, pair_items, items_out, x_low, x_high, z_low, z_high, user_slot, item_slot, request,
+    item_rows, user_rows, items, users, table, sent, came, kept,
 ):
-    y, core, x, z = (lax.axis_index(a) for a in (Y, CORE, X, Z))
+    y, core, _, _ = (lax.axis_index(a) for a in (Y, CORE, X, Z))
     shard, half = items.shape[0], users.shape[0] // 2
     other = {CORE: 1 - core}
     steps = range(1, SIDE)
+    tile = items.shape[1]
+    cut = [pl.ds(k * half * tile, half * tile) for k in range(2)]
+    loads = [pltpu.make_async_copy(item_emb, item_rows, kept.at[3])]
+    loads += [pltpu.make_async_copy(user_emb.at[c], user_rows.at[c], kept.at[4 + k]) for k, c in enumerate(cut)]
+    for copy in loads:
+        copy.start()
     entered = greet([other] + [{a: ahead(a, s)} for a in (Y, X, Z) for s in steps])
-    tile = items.shape[1]
+
+    def cast_users(k):
+        loads[1 + k].wait()
+        for i in range(k * half, (k + 1) * half):
+            users[i] = user_rows[pl.ds(i * tile, tile)].T.astype(jnp.bfloat16)
+
+    loads[0].wait()
     for i in range(shard):
-        items[i] = item_emb[pl.ds(i * tile, tile)].astype(jnp.bfloat16)
-    for i in range(2 * half):
-        users[i] = user_emb[pl.ds(i * tile, tile)].T.astype(jnp.bfloat16)
+        items[i] = item_rows[pl.ds(i * tile, tile)].astype(jnp.bfloat16)
     entered()
 
     def place(y_of, core_of):
@@ -75,20 +86,30 @@
         return copy
 
     ways = {
-        Y: (items, lambda i: place(i, core), 0),
-        X: (users.at[pl.ds(0, half)], lambda i: x_out.at[i], 4),
-        Z: (users.at[pl.ds(half, half)], lambda i: z_out.at[i], 8),
+        Y: (items, lambda i, k: place(i, core).at[pl.ds(k * (shard // 2), shard // 2)]),
+        X: (users.at[pl.ds(0, half)], lambda i, k: (x_low, x_high)[k].at[i]),
+        Z: (users.at[pl.ds(half, half)], lambda i, k: (z_low, z_high)[k].at[i]),
     }
+
+    def parts_of(axis, i):
+        src, spot = ways[axis]
+        size = src.shape[0] // 2
+        return [(src.at[pl.ds(k * size, size)], spot(i, k)) for k in range(2)]
+
     near = {}
-    for axis, (src, spot, base) in ways.items():
-        mine = spot(lax.axis_index(axis))
-        near[axis] = [send(base + k, src, mine, {axis: ahead(axis, s)}) for k, s in enumerate((1, 3))]
-    copies = [send(12, items, place(y, core), other)]
+    for n, axis in enumerate(ways):
+        if axis != Y:
+            cast_users(0 if axis == X else 1)
+        for k, (src, dst) in enumerate(parts_of(axis, lax.axis_index(axis))):
+            for j, s in ((k, (1, 3)[k]), (1 - k, (3, 1)[k])):
+                near[axis, j, k] = send(4 * n + 2 * j + k, src, dst, {axis: ahead(axis, s)})
+    copies = [send(18, items, place(y, core), other)]
     local = [
         pltpu.make_async_copy(items, place(y, core), kept.at[0]),
-        pltpu.make_async_copy(users.at[pl.ds(0, half)], x_out.at[x], kept.at[1]),
-        pltpu.make_async_copy(users.at[pl.ds(half, half)], z_out.at[z], kept.at[2]),
     ]
+    for n, axis in enumerate((X, Z)):
+        for k, (src, dst) in enumerate(parts_of(axis, lax.axis_index(axis))):
+            local.append(pltpu.make_async_copy(src, dst, kept.at[6 + 2 * n + k]))
     for copy in local:
         copy.start()
 
@@ -107,19 +128,21 @@
         request[d] = table[pl.ds(d, 1)]
 
     far = []
-    for axis, (_, spot, base) in ways.items():
-        for k, s in enumerate((1, 3)):
-            near[axis][k].wait()
-            came_in = spot(ahead(axis, SIDE - s))
-            part = came_in.shape[0] // 2
-            part = came_in.at[pl.ds(k * part, part)]
-            far.append(send(base + 2 + k, part, part, {axis: ahead(axis, s)}))
-            if axis == Y:
-                copies.append(send(13 + k, came_in, came_in, other))
-    for k in range(2):
-        far[k].wait()
-        part = place(ahead(Y, 2), core).at[pl.ds(k * (shard // 2), shard // 2)]
-        copies.append(send(15 + k, part, part, other))
+    for n, axis in enumerate(ways):
+        for j, s in enumerate((1, 3)):
+            back = ahead(axis, SIDE - s)
+            near[axis, j, j].wait()
+            part = ways[axis][1](back, j)
+            far.append(send(12 + 2 * n + j, part, part, {axis: ahead(axis, s)}))
+    for j in range(2):
+        near[Y, j, 1 - j].wait()
+        came_in = place(ahead(Y, SIDE - (1, 3)[j]), core)
+        copies.append(send(19 + j, came_in, came_in, other))
+    for j in range(2):
+        far[j].wait()
+        part = ways[Y][1](ahead(Y, 2), j)
+        copies.append(send(21 + j, part, part, other))
+    copies += [near[axis, j, 1 - j] for axis in (X, Z) for j in range(2)]
     copies += far[2:]
     for copy in copies + local:
         copy.wait()
@@ -128,23 +151,24 @@
 def first_gather(item_emb, user_emb, tile, pair_users, pair_items, widths, devices):
     shard, side = item_emb.shape[0] // tile, (tile, item_emb.shape[1])
     half, count = user_emb.shape[0] // tile // 2, pair_users.shape[1]
-    stage = jax.ShapeDtypeStruct((SIDE, half, *side), jnp.bfloat16)
+    stage = jax.ShapeDtypeStruct((SIDE, half // 2, *side), jnp.bfloat16)
     slot = jax.ShapeDtypeStruct((count, 1), jnp.int32)
     return pl.pallas_call(
         functools.partial(first_gather_kernel, widths),
         name="first_gather",
         out_shape=(
-            jax.ShapeDtypeStruct((8 * shard, *side), jnp.bfloat16), stage, stage,
+            jax.ShapeDtypeStruct((8 * shard, *side), jnp.bfloat16), stage, stage, stage, stage,
             slot, slot, jax.ShapeDtypeStruct((devices, 1, 128), jnp.int32),
         ),
-        in_specs=[VMEM] * 4,
-        out_specs=(ANY, ANY, ANY, VMEM, VMEM, VMEM),
+        in_specs=[ANY, ANY, VMEM, VMEM],
+        out_specs=(ANY,) * 5 + (VMEM,) * 3,
         scratch_shapes=[
+            pltpu.VMEM(item_emb.shape, jnp.float32), pltpu.VMEM(user_emb.shape, jnp.float32),
             pltpu.VMEM((shard, *side), jnp.bfloat16), pltpu.VMEM((2 * half, *side), jnp.bfloat16),
-            pltpu.VMEM((devices, 128), jnp.int32), DMA((17,)), DMA((17,)), DMA((3,)),
+            pltpu.VMEM((devices, 128), jnp.int32), DMA((23,)), DMA((23,)), DMA((10,)),
         ],
         compiler_params=pltpu.CompilerParams(
-            collective_id=0, has_side_effects=True, vmem_limit_bytes=58 * 2**20
+            collective_id=0, has_side_effects=True, vmem_limit_bytes=WHOLE
         ),
     )(item_emb, user_emb, pair_users, pair_items)
 
@@ -159,8 +183,8 @@
 
 def settle_kernel(
     devices, each,
-    x_own, x_up, x_down, z_own, z_up, z_down, items, user_emb, item_emb, request, user_slot, item_slot, negatives,
-    user_out, item_out, margin,
+    x_own, x_up, x_down, z_own, z_up, z_down, items, user_from, item_from, request, user_slot, item_slot, negatives,
+    user_to, item_to, user_vec, positive, negative_vec, user_emb, item_emb, user_out, item_out,
     got_x, got_z, sum_x, sum_z, last_x, last_z, got_i, sum_i, last_i, asked, wanted, stage, packs, arrived, chosen_negs,
     sent, came, kept, ready, ask_sent, ask_came, row_sent, row_came,
 ):
@@ -184,7 +208,11 @@
     loads = [pltpu.make_async_copy(ref, got_x.at[k], kept.at[k]) for k, ref in enumerate((x_own, x_up, x_down))]
     loads += [pltpu.make_async_copy(ref, got_z.at[k], kept.at[4 + k]) for k, ref in enumerate((z_own, z_up, z_down))]
     loads.append(pltpu.make_async_copy(items.at[:, core], got_i.at[0], kept.at[8]))
-    for copy in loads:
+    embs = [
+        pltpu.make_async_copy(user_from, user_emb, kept.at[3]),
+        pltpu.make_async_copy(item_from, item_emb, kept.at[7]),
+    ]
+    for copy in loads + embs:
         copy.start()
 
     def send(k, src, dst, peer):
@@ -265,15 +293,24 @@
             copy.wait()
         finish(emb, to, start, [got.at[j, mine] for j in range(parts)] + [final.at[j] for j in range(3)])
 
+    group = y * 2 + core
+    for copy in embs:
+        copy.wait()
     settle_axis(Y, y, item_emb, item_out, 0)
     for k in range(each):
-        stage[0, pl.ds(k, 1)] = item_out[pl.ds(negatives[k], 1)]
-    group = y * 2 + core
+        local = lax.rem(negatives[me * each + k], item_out.shape[0])
+        stage[0, pl.ds(k, 1)] = item_out[pl.ds(local, 1)]
     chosen_negs[group, x, z] = stage[0, pl.ds(0, each)].astype(jnp.bfloat16)
     own = chosen_negs.at[group, x, z]
     first = [send(9 + s, own, own, {X: ahead(X, s)}) for s in steps]
     settle_axis(Z, z, user_emb, user_out, 0)
     settle_axis(X, x, user_emb, user_out, half * tile)
+    stores = [
+        pltpu.make_async_copy(user_out, user_to, kept.at[12]),
+        pltpu.make_async_copy(item_out, item_to, kept.at[13]),
+    ]
+    for copy in stores:
+        copy.start()
     listed.wait()
     for copy in first:
         copy.wait()
@@ -317,15 +354,11 @@
 
     users = picked(user_slot, 0)
     chosen = picked(item_slot, each)
-    positive = jnp.sum(users * chosen, axis=1, keepdims=True)
-    against = chosen_negs[...].reshape(devices * each, -1)
-    margin[...] = (
-        lax.dot_general(
-            users.astype(jnp.bfloat16), against, (((1,), (1,)), ((), ())),
-            preferred_element_type=jnp.float32,
-        )
-        - positive
-    )
+    positive[...] = jnp.sum(users * chosen, axis=1, keepdims=True)
+    user_vec[...] = users.astype(jnp.bfloat16)
+    negative_vec[...] = chosen_negs[...].reshape(devices * each, -1)
+    for copy in stores:
+        copy.wait()
 
 
 def settle(over_x, over_z, items, user_emb, item_emb, request, user_slot, item_slot, negatives):
@@ -333,7 +366,8 @@
     embed = user_emb.shape[1]
     half, shard = over_x[0].shape[1], item_emb.shape[0] // side[0]
     items = items.reshape(SIDE, 2, shard, *side)
-    devices, each, pairs = request.shape[0], negatives.shape[0], user_slot.shape[0]
+    devices, pairs = request.shape[0], user_slot.shape[0]
+    each = negatives.shape[0] // devices
     many, one, low = (SIDE, half, *side), (half, *side), jnp.bfloat16
     return pl.pallas_call(
         functools.partial(settle_kernel, devices, each),
@@ -341,11 +375,15 @@
         out_shape=(
             jax.ShapeDtypeStruct(user_emb.shape, jnp.float32),
             jax.ShapeDtypeStruct(item_emb.shape, jnp.float32),
-            jax.ShapeDtypeStruct((pairs, devices * each), jnp.float32),
+            jax.ShapeDtypeStruct((pairs, embed), low),
+            jax.ShapeDtypeStruct((pairs, 1), jnp.float32),
+            jax.ShapeDtypeStruct((devices * each, embed), low),
         ),
-        in_specs=[ANY] * 7 + [VMEM] * 5 + [SMEM],
-        out_specs=(VMEM,) * 3,
+        in_specs=[ANY] * 9 + [VMEM] * 3 + [SMEM],
+        out_specs=(ANY, ANY, VMEM, VMEM, VMEM),
         scratch_shapes=[
+            pltpu.VMEM(user_emb.shape, jnp.float32), pltpu.VMEM(item_emb.shape, jnp.float32),
+            pltpu.VMEM(user_emb.shape, jnp.float32), pltpu.VMEM(item_emb.shape, jnp.float32),
             pltpu.VMEM((3, *many), low), pltpu.VMEM((3, *many), low),
             pltpu.VMEM((3, *one), low), pltpu.VMEM((3, *one), low),
             pltpu.VMEM((3, *one), low), pltpu.VMEM((3, *one), low),
@@ -355,12 +393,37 @@
             pltpu.VMEM((8, 2 * each, embed), jnp.float32),
             pltpu.VMEM((devices, 2 * each, embed), low), pltpu.VMEM((devices, 2 * each, embed), low),
             pltpu.VMEM((2 * SIDE, SIDE, SIDE, each, embed), low),
-            DMA((27,)), DMA((27,)), DMA((12,)), pltpu.SemaphoreType.REGULAR((2,)), DMA, DMA, DMA, DMA,
+            DMA((27,)), DMA((27,)), DMA((14,)), pltpu.SemaphoreType.REGULAR((2,)), DMA, DMA, DMA, DMA,
         ],
         compiler_params=pltpu.CompilerParams(
-            collective_id=1, has_side_effects=True, vmem_limit_bytes=58 * 2**20
+            collective_id=1, has_side_effects=True, vmem_limit_bytes=WHOLE
         ),
     )(*over_x, *over_z, items, user_emb, item_emb, request, user_slot, item_slot, negatives)
+
+
+def last_kernel(user_vec, positive, negative_vec, users, items, terms, users_out, items_out):
+    margin = lax.dot_general(
+        user_vec[...], negative_vec[...], (((1,), (1,)), ((), ())), preferred_element_type=jnp.float32
+    )
+    terms[...] = jnp.log1p(jnp.exp(margin - positive[...]))
+    users_out[...] = users[...]
+    items_out[...] = items[...]
+
+
+def last(user_vec, positive, negative_vec, users, items, steps=4):
+    def block(array):
+        return pl.BlockSpec((array.shape[0] // steps, array.shape[1]), lambda i: (i, 0))
+
+    terms = jax.ShapeDtypeStruct((user_vec.shape[0], negative_vec.shape[0]), jnp.float32)
+    return pl.pallas_call(
+        last_kernel,
+        name="last",
+        grid=(steps,),
+        out_shape=[terms] + [jax.ShapeDtypeStruct(array.shape, array.dtype) for array in (users, items)],
+        in_specs=[block(user_vec), block(positive), pl.BlockSpec(negative_vec.shape, lambda i: (0, 0)), block(users), block(items)],
+        out_specs=[block(terms), block(users), block(items)],
+        compiler_params=pltpu.CompilerParams(vmem_limit_bytes=WHOLE),
+    )(user_vec, positive, negative_vec, users, items)
 
 
 def joined_kernel(*refs):
@@ -381,7 +444,7 @@
         in_specs=spots + [pl.BlockSpec(block, lambda i: (i, 0, 0, 0))] * 4,
         out_specs=spots,
         input_output_aliases={k: k for k in range(4)},
-        compiler_params=pltpu.CompilerParams(vmem_limit_bytes=58 * 2**20),
+        compiler_params=pltpu.CompilerParams(vmem_limit_bytes=WHOLE),
         cost_estimate=pl.CostEstimate(flops=2**20, bytes_accessed=6 * 2**20, transcendentals=0),
     )(*parts, *relayed)
 
@@ -467,7 +530,7 @@
             DMA,
             DMA,
         ],
-        compiler_params=pltpu.CompilerParams(vmem_limit_bytes=56 * 2**20),
+        compiler_params=pltpu.CompilerParams(vmem_limit_bytes=WHOLE),
         cost_estimate=pl.CostEstimate(
             flops=slots * 2 * side * side * embed,
             bytes_accessed=2 * (vals.size + (held + total) * side * embed),
@@ -498,13 +561,17 @@
     slots = (tile_vals[0, 0], tile_rows[0, 0], tile_cols[0, 0], tile_count[0])
 
     devices = row_count * col_count
-    neg_each = negatives.shape[0] // devices
     user_rows, item_rows = user_emb.reshape(-1, embed), item_emb.reshape(-1, embed)
-    item_tiles, from_x, from_z, user_slot, item_slot, request = first_gather(
+    item_tiles, x_low, x_high, z_low, z_high, user_slot, item_slot, request = first_gather(
         item_rows, user_rows, side, pair_users[None], pair_items[None], (user_dev, item_dev), devices
     )
-    near = [(shifted(array, axis, step), 1 if step == 1 else 3, late, 0)
-            for step in (1, -1) for array, axis, late in ((from_x, Z, 0), (from_z, X, 1))]
+    held = [(x_low, 0, 0, 0), (x_high, 0, 0, 1), (z_low, 0, 1, 0), (z_high, 0, 1, 1)]
+    near = []
+    for first in (True, False):
+        for array, _, late, k in held:
+            step = 1 if (k == 0) == first else -1
+            moved = shifted(array, X if late else Z, step)
+            near.append((moved, SIDE - 1 if step == -1 else 1, late, k))
 
     def item_places(refs):
         return [(refs[0], 0)]
@@ -533,35 +600,30 @@
         for k, step in ((3, 1), (4, -1)):
             relay.append(shifted(user_parts[5 * late + k], axis, step))
     far = []
-    for array, back, late, _ in near:
-        cut = slice(0, SIDE // 2) if back == 1 else slice(SIDE // 2, SIDE)
-        sent_on = shifted(array[cut], X if late else Z, 1 if back == 1 else -1)
-        far.append((sent_on, 2, late, cut.start))
+    for array, back, late, k in near[:4]:
+        sent_on = shifted(array, X if late else Z, 1 if back == 1 else -1)
+        far.append((sent_on, 2, late, k))
     onward = joined([user_parts[k] for k in (1, 2, 6, 7)], relay)
     over_x, over_z = [user_parts[0]], [user_parts[5]]
     for k, (over, axis, step) in enumerate(((over_x, X, 1), (over_x, X, -1), (over_z, Z, 1), (over_z, Z, -1))):
         over.append(shifted(onward[k], axis, step))
-    spread = [(from_x, 0, 0, 0), (from_z, 0, 1, 0)] + near + far
+    spread = held + near + far
 
     def user_places(refs):
-        for ref, (array, back, late, start) in zip(refs, spread):
+        for ref, (array, back, late, k) in zip(refs, spread):
             at = lax.rem(lax.axis_index(X if late else Z) + SIDE - back, SIDE)
-            for i in range(array.shape[0]):
-                holder = at * SIDE + start + i if late else (start + i) * SIDE + at
-                yield ref.at[i], holder * user_each + late * half
+            for i in range(SIDE):
+                holder = at * SIDE + i if late else i * SIDE + at
+                yield ref.at[i], holder * user_each + late * half + k * (half // 2)
 
     (item_part,) = tile_terms(
         False, *slots, [part[0] for part in spread], user_places, user_each * col_count,
         [item_tiles.shape], item_takes,
     )
-    offset = (lax.axis_index(COL) * row_count + lax.axis_index(ROW)) * item_dev
-    device_rank = lax.axis_index(ROW) * col_count + lax.axis_index(COL)
-    mine = lax.dynamic_slice_in_dim(negatives, device_rank * neg_each, neg_each, 0) - offset
-    user_final, item_final, margin = settle(
-        over_x, over_z, item_part, user_rows, item_rows,
-        request, user_slot, item_slot, mine,
+    user_final, item_final, user_vec, positive, negative_vec = settle(
+        over_x, over_z, item_part, user_rows, item_rows, request, user_slot, item_slot, negatives
     )
-    bpr_terms = jnp.log1p(jnp.exp(margin))
+    bpr_terms, user_final, item_final = last(user_vec, positive, negative_vec, user_final, item_final)
     return (user_final.reshape(user_emb.shape), item_final.reshape(item_emb.shape), bpr_terms)
 
 

time: 202 us -> 179 us (0.89)
  waiting for transfers between devices: 59.4 us -> 42 us
  local copies, waits for them, and re-layouts: 11.7 us -> 0 us
  starting transfers between devices: 22.7 us -> 31.2 us
    ppermute x16 -> x20, waiting for transfers between devices: 59.4 us -> 42 us  [shifted(): lax.ppermute(array, axis, [(i, (i + step) % SIDE) for i in range(SIDE)])]
    ppermute x16 -> x20, starting transfers between devices: 22.7 us -> 31.2 us  [shifted(): lax.ppermute(array, axis, [(i, (i + step) % SIDE) for i in range(SIDE)])]
    pallas_call x0 -> x1, Pallas kernels: none -> 4.82 us  [last(): pl.pallas_call(last_kernel, name='last', grid=(steps,), out_shape=[terms]...]
    unnamed x34 -> x0, local copies, waits for them, and re-layouts: 4.59 us -> none
    pallas_call x1, Pallas kernels: 54.7 us -> 50.4 us  [settle(): pl.pallas_call(functools.partial(settle_kernel, devices, each), name='set...]
    log1p x1 -> x0, local copies, waits for them, and re-layouts: 3.77 us -> none  [on_device(): bpr_terms = jnp.log1p(jnp.exp(margin))]
    slice x4 -> x0, local copies, waits for them, and re-layouts: 3.36 us -> none  [on_device(): sent_on = shifted(array[cut], X if late else Z, 1 if back == 1 else -1)]
  transfers between devices with their start and end apart: 16 -> 20, of which waited for: 5 -> 6; matrix products, arithmetic and copies ran while one was open for 2% -> 0% of each run, Pallas kernels for 14% -> 15%
where the time goes in v4:
time: 179 us
  Pallas kernels  104 us (58%)
  waiting for transfers between devices  42 us (23%)
  starting transfers between devices  31.2 us (17%)
    pallas_call x1, Pallas kernels, settle(): pl.pallas_call(functools.partial(settle_kernel, devices, each), name='set...  50.4 us
    ppermute x20, waiting for transfers between devices, shifted(): lax.ppermute(array, axis, [(i, (i + step) % SIDE) for i in range(SIDE)])  42 us
    ppermute x20, starting transfers between devices, shifted(): lax.ppermute(array, axis, [(i, (i + step) % SIDE) for i in range(SIDE)])  31.2 us
    pallas_call x2, Pallas kernels, tile_terms(): pl.pallas_call(functools.partial(tile_kernel, width, depth, users, place,...  24 us
    pallas_call x1, Pallas kernels, first_gather(): pl.pallas_call(functools.partial(first_gather_kernel, widths), name='firs...  21.4 us
    pallas_call x1, Pallas kernels, last(): pl.pallas_call(last_kernel, name='last', grid=(steps,), out_shape=[terms]...  4.82 us
  transfers between devices with their start and end apart: 20, of which 6 were waited for; matrix products, arithmetic and copies ran while one was open for 0% of the time, Pallas kernels for 15%

profile of v4, /device:TPU:1, one launch (start us, length us, event | category | flops | bytes accessed | tf_op | source)
XLA Modules:
  0.0 178.5 jit_solution(3491480544171386284)
XLA Ops:
  0.6 21.4 %first_gather.1 = (bf16[64,128,128]{2,1,0:T(8,128)(2,1)}, bf16[4,4,128,128]{3,2,1,0:T(8,128)(2,1)}, bf16[4,4,128,128]{3,2,1,0:T(8,128)(2,1)}, bf16[4,4,128,128]{...) custom-call(f32[1024,128]{1,0:T(8,128)} %bitcast.18, ...), custom_call_target="tpu_custom_call" | custom-call | tf_op jit(solution)/shard_map/first_gather/pallas_call | solution.py:156
  22.0 2.8 %collective-permute-start.12 = (bf16[4,4,128,128]{3,2,1,0:T(8,128)(2,1)}, bf16[4,4,128,128]{3,2,1,0:T(8,128)(2,1)}, u32[]{:S(2)}, u32[]{:S(2)}) collective-permute-start(bf16[4,4,128,128]{3,2,1,0:T(8,128)(2,1)} %get-tuple-element.48.refs_0_), channel_id=1, source_target_pairs={{0,3},{1,0},{2,1},{3,2},{4,7},{5,4},{6,5},{7,6},{8,11},{9,8},{10,9... | collective-permute-start | bytes 1572872 | tf_op jit(solution)/shard_map/ppermute | solution.py:177
  24.8 2.7 %collective-permute-start.9 = (bf16[4,4,128,128]{3,2,1,0:T(8,128)(2,1)}, bf16[4,4,128,128]{3,2,1,0:T(8,128)(2,1)}, u32[]{:S(2)}, u32[]{:S(2)}) collective-permute-start(bf16[4,4,128,128]{3,2,1,0:T(8,128)(2,1)} %get-tuple-element.49.refs_1_), channel_id=1, source_target_pairs={{0,3},{1,0},{2,1},{3,2},{4,7},{5,4},{6,5},{7,6},{8,11},{9,8},{10,9... | collective-permute-start | bytes 1572872 | tf_op jit(solution)/shard_map/ppermute | solution.py:177
  27.5 1.2 collective-permute-start.14
  29.4 6.9 %collective-permute-done.12.refs_8_ = bf16[4,4,128,128]{3,2,1,0:T(8,128)(2,1)} collective-permute-done((bf16[4,4,128,128]{3,2,1,0:T(8,128)(2,1)}, bf16[4,4,128,128]{3,2,1,0:T(8,128)(2,1)}, u32[]{:S(2)}, u32[]{:S(2)}) %collective-permute-start.12) | collective-permute-done | bytes 524320 | tf_op jit(solution)/shard_map/ppermute | solution.py:177
  36.6 8.8 %user_terms.1 = (bf16[4,8,128,128]{3,2,1,0:T(8,128)(2,1)}, bf16[4,8,128,128]{3,2,1,0:T(8,128)(2,1)}, bf16[4,8,128,128]{3,2,1,0:T(8,128)(2,1)}, bf16[2,8,128,128]...) custom-call(s32[1]{0:T(128)} %bitcast.11.count_ref, ...), custom_call_target="tpu_custom_call" | custom-call | flops 2147483648 | bytes 27262976 | tf_op jit(solution)/shard_map/user_terms/pallas_call | solution.py:518
  45.4 4.2 %collective-permute-start = (bf16[2,8,128,128]{3,2,1,0:T(8,128)(2,1)}, bf16[2,8,128,128]{3,2,1,0:T(8,128)(2,1)}, u32[]{:S(2)}, u32[]{:S(2)}) collective-permute-start(bf16[2,8,128,128]{3,2,1,0:T(8,128)(2,1)} %get-tuple-element.39), channel_id=1, source_target_pairs={{0,4},{4,8},{8,12},{12,0},{1,5},{5,9},{9,13},{13,1},{2,6},{6,10},{... | collective-permute-start | bytes 1572872 | tf_op jit(solution)/shard_map/ppermute | solution.py:177
  49.6 1.0 collective-permute-done.13.refs_9_
  50.6 0.9 collective-permute-start.1
  51.5 1.9 %collective-permute-start.2 = (bf16[2,8,128,128]{3,2,1,0:T(8,128)(2,1)}, bf16[2,8,128,128]{3,2,1,0:T(8,128)(2,1)}, u32[]{:S(2)}, u32[]{:S(2)}) collective-permute-start(bf16[2,8,128,128]{3,2,1,0:T(8,128)(2,1)} %get-tuple-element.41), channel_id=1, source_target_pairs={{0,1},{1,2},{2,3},{3,0},{4,5},{5,6},{6,7},{7,4},{8,9},{9,10},{10,1... | collective-permute-start | bytes 1572872 | tf_op jit(solution)/shard_map/ppermute | solution.py:177
  53.4 2.5 %collective-permute-start.3 = (bf16[2,8,128,128]{3,2,1,0:T(8,128)(2,1)}, bf16[2,8,128,128]{3,2,1,0:T(8,128)(2,1)}, u32[]{:S(2)}, u32[]{:S(2)}) collective-permute-start(bf16[2,8,128,128]{3,2,1,0:T(8,128)(2,1)} %get-tuple-element.42), channel_id=1, source_target_pairs={{0,3},{1,0},{2,1},{3,2},{4,7},{5,4},{6,5},{7,6},{8,11},{9,8},{10,9... | collective-permute-start | bytes 1572872 | tf_op jit(solution)/shard_map/ppermute | solution.py:177
  56.0 2.7 %collective-permute-done.refs_4_ = bf16[2,8,128,128]{3,2,1,0:T(8,128)(2,1)} collective-permute-done((bf16[2,8,128,128]{3,2,1,0:T(8,128)(2,1)}, bf16[2,8,128,128]{3,2,1,0:T(8,128)(2,1)}, u32[]{:S(2)}, u32[]{:S(2)}) %collective-permute-start) | collective-permute-done | bytes 524320 | tf_op jit(solution)/shard_map/ppermute | solution.py:177
  58.7 1.1 collective-permute-start.11
  59.8 2.8 %collective-permute-done.1.refs_5_ = bf16[2,8,128,128]{3,2,1,0:T(8,128)(2,1)} collective-permute-done((bf16[2,8,128,128]{3,2,1,0:T(8,128)(2,1)}, bf16[2,8,128,128]{3,2,1,0:T(8,128)(2,1)}, u32[]{:S(2)}, u32[]{:S(2)}) %collective-permute-start.1) | collective-permute-done | bytes 524320 | tf_op jit(solution)/shard_map/ppermute | solution.py:177
  62.6 3.6 %collective-permute-start.16 = (bf16[4,4,128,128]{3,2,1,0:T(8,128)(2,1)}, bf16[4,4,128,128]{3,2,1,0:T(8,128)(2,1)}, u32[]{:S(2)}, u32[]{:S(2)}) collective-permute-start(bf16[4,4,128,128]{3,2,1,0:T(8,128)(2,1)} %collective-permute-done.8.refs_4_), channel_id=1, source_target_pairs={{0,1},{1,2},{2,3},{3,0},{4,5},{5,6},{6,7},{7,4},{8,9},{9,10},{10,1... | collective-permute-start | bytes 1572872 | tf_op jit(solution)/shard_map/ppermute | solution.py:177
  66.2 3.7 %collective-permute-start.17 = (bf16[4,4,128,128]{3,2,1,0:T(8,128)(2,1)}, bf16[4,4,128,128]{3,2,1,0:T(8,128)(2,1)}, u32[]{:S(2)}, u32[]{:S(2)}) collective-permute-start(bf16[4,4,128,128]{3,2,1,0:T(8,128)(2,1)} %collective-permute-done.9.refs_5_), channel_id=1, source_target_pairs={{0,3},{1,0},{2,1},{3,2},{4,7},{5,4},{6,5},{7,6},{8,11},{9,8},{10,9... | collective-permute-start | bytes 1572872 | tf_op jit(solution)/shard_map/ppermute | solution.py:177
  70.2 3.3 %joined.1 = (bf16[4,8,128,128]{3,2,1,0:T(8,128)(2,1)}, bf16[4,8,128,128]{3,2,1,0:T(8,128)(2,1)}, bf16[4,8,128,128]{3,2,1,0:T(8,128)(2,1)}, bf16[4,8,128,128]{3,2,1,0:T(8,128)(2,1)}) custom-call(bf16[4,8,128,128]{3,2,1,0:T(8,128)(2,1)} %get-tuple-element.35.refs_0_, ...), custom_call_target="tpu_custom_call", output_to_operand_aliasing={{0}: (0, {}), {1}: (1, {}), {2}: (2, {}), {3}: (3, {})} | custom-call | flops 1048576 | bytes 6291456 | tf_op jit(solution)/shard_map/joined/pallas_call | solution.py:439
  73.6 2.7 %collective-permute-start.5 = (bf16[4,8,128,128]{3,2,1,0:T(8,128)(2,1)}, bf16[4,8,128,128]{3,2,1,0:T(8,128)(2,1)}, u32[]{:S(2)}, u32[]{:S(2)}) collective-permute-start(bf16[4,8,128,128]{3,2,1,0:T(8,128)(2,1)} %get-tuple-element.44), channel_id=1, source_target_pairs={{0,12},{4,0},{8,4},{12,8},{1,13},{5,1},{9,5},{13,9},{2,14},{6,2},{... | collective-permute-start | bytes 3145736 | tf_op jit(solution)/shard_map/ppermute | solution.py:177
  76.3 4.8 %collective-permute-done.16.refs_12_ = bf16[4,4,128,128]{3,2,1,0:T(8,128)(2,1)} collective-permute-done((bf16[4,4,128,128]{3,2,1,0:T(8,128)(2,1)}, bf16[4,4,128,128]{3,2,1,0:T(8,128)(2,1)}, u32[]{:S(2)}, u32[]{:S(2)}) %collective-permute-start.16) | collective-permute-done | bytes 524320 | tf_op jit(solution)/shard_map/ppermute | solution.py:177
  81.1 2.7 %collective-permute-start.7 = (bf16[4,8,128,128]{3,2,1,0:T(8,128)(2,1)}, bf16[4,8,128,128]{3,2,1,0:T(8,128)(2,1)}, u32[]{:S(2)}, u32[]{:S(2)}) collective-permute-start(bf16[4,8,128,128]{3,2,1,0:T(8,128)(2,1)} %get-tuple-element.47), channel_id=1, source_target_pairs={{0,3},{1,0},{2,1},{3,2},{4,7},{5,4},{6,5},{7,6},{8,11},{9,8},{10,9... | collective-permute-start | bytes 3145736 | tf_op jit(solution)/shard_map/ppermute | solution.py:177
  84.3 23.7 %collective-permute-done.19.refs_15_ = bf16[4,4,128,128]{3,2,1,0:T(8,128)(2,1)} collective-permute-done((bf16[4,4,128,128]{3,2,1,0:T(8,128)(2,1)}, bf16[4,4,128,128]{3,2,1,0:T(8,128)(2,1)}, u32[]{:S(2)}, u32[]{:S(2)}) %collective-permute-start.19) | collective-permute-done | bytes 524320 | tf_op jit(solution)/shard_map/ppermute | solution.py:177
  108.0 15.2 %item_terms.1 = bf16[64,128,128]{2,1,0:T(8,128)(2,1)} custom-call(s32[1]{0:T(128)} %bitcast.12.count_ref, s32[512]{0:T(512)} %bitcast.21, s32[512]{0:T(512)} %bitcast.23, bf16[512,128,128]{2,1,0:T(8,128)(2,1)} %bitcast.14, bf16[4,4,128,128]{3,2,1,0:T(8,128)(2,1)} %get-tuple-element.48.refs_0_, bf16[4,4,128,128]{3,2,1,0:T(8,128)(2,1)} %get-tuple-element.49.refs_1_, ...), custom_call_target="tpu_custom_call" | custom-call | flops 2147483648 | bytes 27262976 | tf_op jit(solution)/shard_map/item_terms/pallas_call | solution.py:518
  123.2 50.4 %settle.1 = (f32[2048,128]{1,0:T(8,128)}, f32[1024,128]{1,0:T(8,128)}, bf16[512,128]{1,0:T(8,128)(2,1)}, f32[512,1]{1,0:T(8,128)}, bf16[1024,128]{1,0:T(8,128)(2,1)}) custom-call(bf16[4,8,128,128]{3,2,1,0:T(8,128)(2,1)} %get-tuple-element.34.x_own, bf16[4,8,128,128]{3,2,1,0:T(8,128)(2,1)} %collective-permute-done.4.x_up, ...), custom_call_target="tpu_custom_call" | custom-call | tf_op jit(solution)/shard_map/settle/pallas_call | solution.py:372
  173.7 4.8 %last.1 = (f32[512,1024]{1,0:T(8,128)}, f32[2048,128]{1,0:T(8,128)}, f32[1024,128]{1,0:T(8,128)}) custom-call(bf16[512,128]{1,0:T(8,128)(2,1)} %get-tuple-element.55.user_vec, f32[512,1]{1,0:T(8,128)} %get-tuple-element.56.positive, bf16[1024,128]{1,0:T(8,128)(2,1)} %get-tuple-element.57.negative_vec, f32[2048,128]{1,0:T(8,128)} %get-tuple-element.58.users, ...), custom_call_target="tpu_custom_call" | custom-call | tf_op jit(solution)/shard_map/last/pallas_call | solution.py:418
  (22 shorter events, 1.3 us)
Async XLA Ops:
  22.0 14.3 %collective-permute-start.12 = (bf16[4,4,128,128]{3,2,1,0:T(8,128)(2,1)}, bf16[4,4,128,128]{3,2,1,0:T(8,128)(2,1)}, u32[]{:S(2)}, u32[]{:S(2)}) collective-permute-start(bf16[4,4,128,128]{3,2,1,0:T(8,128)(2,1)} %get-tuple-element.48.refs_0_), channel_id=1, source_target_pairs={{0,3},{1,0},{2,1},{3,2},{4,7},{5,4},{6,5},{7,6},{8,11},{9,8},{10,9... | collective-permute-start | bytes 1572872 | tf_op jit(solution)/shard_map/ppermute | solution.py:177
  24.8 20.6 %collective-permute-start.8 = (bf16[4,4,128,128]{3,2,1,0:T(8,128)(2,1)}, bf16[4,4,128,128]{3,2,1,0:T(8,128)(2,1)}, u32[]{:S(2)}, u32[]{:S(2)}) collective-permute-start(bf16[4,4,128,128]{3,2,1,0:T(8,128)(2,1)} %get-tuple-element.48.refs_0_), channel_id=1, source_target_pairs={{0,1},{1,2},{2,3},{3,0},{4,5},{5,6},{6,7},{7,4},{8,9},{9,10},{10,1... | collective-permute-start | bytes 1572872 | tf_op jit(solution)/shard_map/ppermute | solution.py:177
  24.8 25.8 %collective-permute-start.13 = (bf16[4,4,128,128]{3,2,1,0:T(8,128)(2,1)}, bf16[4,4,128,128]{3,2,1,0:T(8,128)(2,1)}, u32[]{:S(2)}, u32[]{:S(2)}) collective-permute-start(bf16[4,4,128,128]{3,2,1,0:T(8,128)(2,1)} %get-tuple-element.49.refs_1_), channel_id=1, source_target_pairs={{0,1},{1,2},{2,3},{3,0},{4,5},{5,6},{6,7},{7,4},{8,9},{9,10},{10,1... | collective-permute-start | bytes 1572872 | tf_op jit(solution)/shard_map/ppermute | solution.py:177
  24.8 26.7 %collective-permute-start.9 = (bf16[4,4,128,128]{3,2,1,0:T(8,128)(2,1)}, bf16[4,4,128,128]{3,2,1,0:T(8,128)(2,1)}, u32[]{:S(2)}, u32[]{:S(2)}) collective-permute-start(bf16[4,4,128,128]{3,2,1,0:T(8,128)(2,1)} %get-tuple-element.49.refs_1_), channel_id=1, source_target_pairs={{0,3},{1,0},{2,1},{3,2},{4,7},{5,4},{6,5},{7,6},{8,11},{9,8},{10,9... | collective-permute-start | bytes 1572872 | tf_op jit(solution)/shard_map/ppermute | solution.py:177
  27.5 25.9 %collective-permute-start.14 = (bf16[4,4,128,128]{3,2,1,0:T(8,128)(2,1)}, bf16[4,4,128,128]{3,2,1,0:T(8,128)(2,1)}, u32[]{:S(2)}, u32[]{:S(2)}) collective-permute-start(bf16[4,4,128,128]{3,2,1,0:T(8,128)(2,1)} %get-tuple-element.50.refs_2_), channel_id=1, source_target_pairs={{0,12},{4,0},{8,4},{12,8},{1,13},{5,1},{9,5},{13,9},{2,14},{6,2},{... | collective-permute-start | bytes 1572872 | tf_op jit(solution)/shard_map/ppermute | solution.py:177
  36.3 19.7 %collective-permute-start.10 = (bf16[4,4,128,128]{3,2,1,0:T(8,128)(2,1)}, bf16[4,4,128,128]{3,2,1,0:T(8,128)(2,1)}, u32[]{:S(2)}, u32[]{:S(2)}) collective-permute-start(bf16[4,4,128,128]{3,2,1,0:T(8,128)(2,1)} %get-tuple-element.50.refs_2_), channel_id=1, source_target_pairs={{0,4},{4,8},{8,12},{12,0},{1,5},{5,9},{9,13},{13,1},{2,6},{6,10},{... | collective-permute-start | bytes 1572872 | tf_op jit(solution)/shard_map/ppermute | solution.py:177
  45.4 13.2 %collective-permute-start = (bf16[2,8,128,128]{3,2,1,0:T(8,128)(2,1)}, bf16[2,8,128,128]{3,2,1,0:T(8,128)(2,1)}, u32[]{:S(2)}, u32[]{:S(2)}) collective-permute-start(bf16[2,8,128,128]{3,2,1,0:T(8,128)(2,1)} %get-tuple-element.39), channel_id=1, source_target_pairs={{0,4},{4,8},{8,12},{12,0},{1,5},{5,9},{9,13},{13,1},{2,6},{6,10},{... | collective-permute-start | bytes 1572872 | tf_op jit(solution)/shard_map/ppermute | solution.py:177
  50.6 12.0 %collective-permute-start.1 = (bf16[2,8,128,128]{3,2,1,0:T(8,128)(2,1)}, bf16[2,8,128,128]{3,2,1,0:T(8,128)(2,1)}, u32[]{:S(2)}, u32[]{:S(2)}) collective-permute-start(bf16[2,8,128,128]{3,2,1,0:T(8,128)(2,1)} %get-tuple-element.40), channel_id=1, source_target_pairs={{0,12},{4,0},{8,4},{12,8},{1,13},{5,1},{9,5},{13,9},{2,14},{6,2},{... | collective-permute-start | bytes 1572872 | tf_op jit(solution)/shard_map/ppermute | solution.py:177
  51.5 14.7 %collective-permute-start.2 = (bf16[2,8,128,128]{3,2,1,0:T(8,128)(2,1)}, bf16[2,8,128,128]{3,2,1,0:T(8,128)(2,1)}, u32[]{:S(2)}, u32[]{:S(2)}) collective-permute-start(bf16[2,8,128,128]{3,2,1,0:T(8,128)(2,1)} %get-tuple-element.41), channel_id=1, source_target_pairs={{0,1},{1,2},{2,3},{3,0},{4,5},{5,6},{6,7},{7,4},{8,9},{9,10},{10,1... | collective-permute-start | bytes 1572872 | tf_op jit(solution)/shard_map/ppermute | solution.py:177
  53.4 16.5 %collective-permute-start.3 = (bf16[2,8,128,128]{3,2,1,0:T(8,128)(2,1)}, bf16[2,8,128,128]{3,2,1,0:T(8,128)(2,1)}, u32[]{:S(2)}, u32[]{:S(2)}) collective-permute-start(bf16[2,8,128,128]{3,2,1,0:T(8,128)(2,1)} %get-tuple-element.42), channel_id=1, source_target_pairs={{0,3},{1,0},{2,1},{3,2},{4,7},{5,4},{6,5},{7,6},{8,11},{9,8},{10,9... | collective-permute-start | bytes 1572872 | tf_op jit(solution)/shard_map/ppermute | solution.py:177
  56.0 17.6 %collective-permute-start.15 = (bf16[4,4,128,128]{3,2,1,0:T(8,128)(2,1)}, bf16[4,4,128,128]{3,2,1,0:T(8,128)(2,1)}, u32[]{:S(2)}, u32[]{:S(2)}) collective-permute-start(bf16[4,4,128,128]{3,2,1,0:T(8,128)(2,1)} %get-tuple-element.51.refs_3_), channel_id=1, source_target_pairs={{0,4},{4,8},{8,12},{12,0},{1,5},{5,9},{9,13},{13,1},{2,6},{6,10},{... | collective-permute-start | bytes 1572872 | tf_op jit(solution)/shard_map/ppermute | solution.py:177
  58.7 14.9 %collective-permute-start.11 = (bf16[4,4,128,128]{3,2,1,0:T(8,128)(2,1)}, bf16[4,4,128,128]{3,2,1,0:T(8,128)(2,1)}, u32[]{:S(2)}, u32[]{:S(2)}) collective-permute-start(bf16[4,4,128,128]{3,2,1,0:T(8,128)(2,1)} %get-tuple-element.51.refs_3_), channel_id=1, source_target_pairs={{0,12},{4,0},{8,4},{12,8},{1,13},{5,1},{9,5},{13,9},{2,14},{6,2},{... | collective-permute-start | bytes 1572872 | tf_op jit(solution)/shard_map/ppermute | solution.py:177
  62.6 18.5 %collective-permute-start.16 = (bf16[4,4,128,128]{3,2,1,0:T(8,128)(2,1)}, bf16[4,4,128,128]{3,2,1,0:T(8,128)(2,1)}, u32[]{:S(2)}, u32[]{:S(2)}) collective-permute-start(bf16[4,4,128,128]{3,2,1,0:T(8,128)(2,1)} %collective-permute-done.8.refs_4_), channel_id=1, source_target_pairs={{0,1},{1,2},{2,3},{3,0},{4,5},{5,6},{6,7},{7,4},{8,9},{9,10},{10,1... | collective-permute-start | bytes 1572872 | tf_op jit(solution)/shard_map/ppermute | solution.py:177
  66.2 14.9 %collective-permute-start.17 = (bf16[4,4,128,128]{3,2,1,0:T(8,128)(2,1)}, bf16[4,4,128,128]{3,2,1,0:T(8,128)(2,1)}, u32[]{:S(2)}, u32[]{:S(2)}) collective-permute-start(bf16[4,4,128,128]{3,2,1,0:T(8,128)(2,1)} %collective-permute-done.9.refs_5_), channel_id=1, source_target_pairs={{0,3},{1,0},{2,1},{3,2},{4,7},{5,4},{6,5},{7,6},{8,11},{9,8},{10,9... | collective-permute-start | bytes 1572872 | tf_op jit(solution)/shard_map/ppermute | solution.py:177
  69.9 13.9 %collective-permute-start.18 = (bf16[4,4,128,128]{3,2,1,0:T(8,128)(2,1)}, bf16[4,4,128,128]{3,2,1,0:T(8,128)(2,1)}, u32[]{:S(2)}, u32[]{:S(2)}) collective-permute-start(bf16[4,4,128,128]{3,2,1,0:T(8,128)(2,1)} %collective-permute-done.10.refs_6_), channel_id=1, source_target_pairs={{0,4},{4,8},{8,12},{12,0},{1,5},{5,9},{9,13},{13,1},{2,6},{6,10},{... | collective-permute-start | bytes 1572872 | tf_op jit(solution)/shard_map/ppermute | solution.py:177
  73.5 49.7 %collective-permute-start.4 = (bf16[4,8,128,128]{3,2,1,0:T(8,128)(2,1)}, bf16[4,8,128,128]{3,2,1,0:T(8,128)(2,1)}, u32[]{:S(2)}, u32[]{:S(2)}) collective-permute-start(bf16[4,8,128,128]{3,2,1,0:T(8,128)(2,1)} %get-tuple-element.43), channel_id=1, source_target_pairs={{0,4},{4,8},{8,12},{12,0},{1,5},{5,9},{9,13},{13,1},{2,6},{6,10},{... | collective-permute-start | bytes 3145736 | tf_op jit(solution)/shard_map/ppermute | solution.py:177
  73.6 49.6 %collective-permute-start.5 = (bf16[4,8,128,128]{3,2,1,0:T(8,128)(2,1)}, bf16[4,8,128,128]{3,2,1,0:T(8,128)(2,1)}, u32[]{:S(2)}, u32[]{:S(2)}) collective-permute-start(bf16[4,8,128,128]{3,2,1,0:T(8,128)(2,1)} %get-tuple-element.44), channel_id=1, source_target_pairs={{0,12},{4,0},{8,4},{12,8},{1,13},{5,1},{9,5},{13,9},{2,14},{6,2},{... | collective-permute-start | bytes 3145736 | tf_op jit(solution)/shard_map/ppermute | solution.py:177
  81.1 42.1 %collective-permute-start.6 = (bf16[4,8,128,128]{3,2,1,0:T(8,128)(2,1)}, bf16[4,8,128,128]{3,2,1,0:T(8,128)(2,1)}, u32[]{:S(2)}, u32[]{:S(2)}) collective-permute-start(bf16[4,8,128,128]{3,2,1,0:T(8,128)(2,1)} %get-tuple-element.46), channel_id=1, source_target_pairs={{0,1},{1,2},{2,3},{3,0},{4,5},{5,6},{6,7},{7,4},{8,9},{9,10},{10,1... | collective-permute-start | bytes 3145736 | tf_op jit(solution)/shard_map/ppermute | solution.py:177
  81.1 42.1 %collective-permute-start.7 = (bf16[4,8,128,128]{3,2,1,0:T(8,128)(2,1)}, bf16[4,8,128,128]{3,2,1,0:T(8,128)(2,1)}, u32[]{:S(2)}, u32[]{:S(2)}) collective-permute-start(bf16[4,8,128,128]{3,2,1,0:T(8,128)(2,1)} %get-tuple-element.47), channel_id=1, source_target_pairs={{0,3},{1,0},{2,1},{3,2},{4,7},{5,4},{6,5},{7,6},{8,11},{9,8},{10,9... | collective-permute-start | bytes 3145736 | tf_op jit(solution)/shard_map/ppermute | solution.py:177
  83.8 24.2 %collective-permute-start.19 = (bf16[4,4,128,128]{3,2,1,0:T(8,128)(2,1)}, bf16[4,4,128,128]{3,2,1,0:T(8,128)(2,1)}, u32[]{:S(2)}, u32[]{:S(2)}) collective-permute-start(bf16[4,4,128,128]{3,2,1,0:T(8,128)(2,1)} %collective-permute-done.11.refs_7_), channel_id=1, source_target_pairs={{0,12},{4,0},{8,4},{12,8},{1,13},{5,1},{9,5},{13,9},{2,14},{6,2},{... | collective-permute-start | bytes 1572872 | tf_op jit(solution)/shard_map/ppermute | solution.py:177
